TPU v7x, 256 devices: a whole 4x4x8 slice. The times are simulated.
256 devices in a mesh: ka: 16 (over x, z_hi), pts: 16 (over z_lo, y, core).
Axes of the slice: x: 4, y: 4, z: 8 (z_hi: 4, z_lo: 2; z = z_hi * 2 + z_lo), core: 2. Of those that a mesh axis runs over, the one named last changes fastest.
Arguments:
- valence: bfloat16 [16, 32, 4096], P('ka', None, 'pts'), may hold values from -0.09375 to 0.09375
- conduction: bfloat16 [16, 32, 4096], P('ka', None, 'pts'), may hold values from -6 to 6
- trials: bfloat16 [16, 32, 256], P('ka'), may hold values from -6 to 6
- w_panels: bfloat16 [16, 4096, 4096], P('ka', 'pts'), may hold values from -0.109375 to 0.109375
- partner: int32 [3, 16], replicated, may hold values from 0 to 15, as said below
- owner: int32 [3], replicated, may hold values from 0 to 15, as said below
Outputs:
- applied: float32 [16, 32, 256], P('ka', None, 'pts')
Inputs may be any that keep to these rules, and one draw needn't show every extreme that they name: For each q there is a displacement d with partner[q, k] = (k + d) mod 16 for every k; the 3 displacements differ, are not 0, and include 16 - 1 and 8. `owner`: the 3 entries differ.
All inputs are finite; a program needn't handle non-finite values.
Results may differ from a plain program's by a relative error of at most 0.005.
Values may be sent and summed in bfloat16 or wider, within the bound.
No kernel may reach another device: no remote copies, remote signals or barrier semaphores. Data moves between devices by JAX's collectives and lax.ppermute only.
A program may use at most 64 MiB of HBM per device.

v0:
```python
import jax
import jax.numpy as jnp
from jax import lax
from jax.sharding import PartitionSpec as P


def broadcast(shard, axis, root):
    mine = lax.axis_index(axis) == root
    return lax.psum(jnp.where(mine, shard, jnp.zeros_like(shard)), axis)


def kernel_term(far_cond, far_val, far_trial, panel, own_cond, own_full, ntrial):
    bands = far_trial.shape[0]
    conds = far_cond.shape[0]
    shaped = far_trial.reshape(bands, conds, ntrial)
    block = jnp.einsum("cm,vct->tmv", far_cond, shaped, preferred_element_type=jnp.float32).astype(
        jnp.bfloat16
    )
    image = jnp.einsum("tmv,vn->tmn", block, far_val, preferred_element_type=jnp.float32)
    weighted = (panel.astype(jnp.float32)[None] * image).astype(jnp.bfloat16)
    back = jnp.einsum("tmn,wn->tmw", weighted, own_full, preferred_element_type=jnp.float32)
    part_sum = jnp.einsum(
        "cm,tmw->wct", own_cond.astype(jnp.float32), back, preferred_element_type=jnp.float32
    )
    return part_sum.reshape(bands, conds * ntrial)


def shards(valence, conduction, trials, w_panels, partner, owner):
    nq = partner.shape[0]
    npoint = lax.axis_size("pts")
    here = lax.axis_index("ka")
    bands = valence.shape[1]
    conds = conduction.shape[1]
    ntrial = trials.shape[2] // conds
    own_full = lax.all_gather(valence, "pts", axis=2, tiled=True)
    everyone = (
        lax.all_gather(own_full, "ka", axis=0, tiled=True),
        lax.all_gather(conduction, "ka", axis=0, tiled=True),
        lax.all_gather(trials, "ka", axis=0, tiled=True),
    )
    result = jnp.zeros((bands, conds * ntrial // npoint), jnp.float32)
    for q in range(nq):
        target = partner[q, here]
        far_val = lax.dynamic_index_in_dim(everyone[0], target, 0, keepdims=False)
        far_cond = lax.dynamic_index_in_dim(everyone[1], target, 0, keepdims=False)
        far_trial = lax.dynamic_index_in_dim(everyone[2], target, 0, keepdims=False)
        panel = broadcast(w_panels, "ka", owner[q])[0]
        term = kernel_term(far_cond, far_val, far_trial, panel, conduction[0], own_full[0], ntrial)
        result = result + lax.psum_scatter(term, "pts", scatter_dimension=1, tiled=True)
    return result[None]


def solution(mesh):
    placed = (
        P("ka", None, "pts"),
        P("ka", None, "pts"),
        P("ka", None, None),
        P("ka", "pts", None),
        P(),
        P(),
    )
    return jax.shard_map(
        shards, mesh=mesh, in_specs=placed, out_specs=P("ka", None, "pts"), check_vma=False
    )
```

profile of v0, /device:TPU:2, one launch (start us, length us, event | category | flops | bytes accessed | tf_op | source)
XLA Modules:
  0.0 506.9 jit_solution(3311863029463102849)
XLA Ops:
  6.5 0.0 all-reduce.3.cloned.1.call-start
  6.5 1.3 fusion.56
  9.7 4.4 select_bitcast_fusion
  14.1 0.0 copy-start.4
  14.1 0.0 copy-start.6
  14.1 0.0 copy-start.5
  14.1 0.0 copy-start.3
  14.1 0.0 all-reduce.3.cloned.1.call-update
  14.1 0.0 all-gather.2.cloned.1.call-start
  14.2 0.6 copy-done.4
  14.8 23.0 %all_gather.14 = bf16[1,32,4096]{2,1,0:T(8,128)(2,1)} all-gather(bf16[1,32,256]{2,1,0:T(8,128)(2,1)S(1)} %copy-done.4), channel_id=1, replica_groups=mesh['ka'=16,'pts'=16] {'pts'}, dimensions={2}, use_global_device_ids=true | all-gather | bytes 278528 | tf_op jit(solution)/shard_map/all_gather | solution.py:35
  37.8 0.0 all-gather.2.cloned.1.call-update
  37.8 0.0 reduce-scatter.2.cloned.1.call-start
  37.9 0.0 copy-done.6
  37.9 0.7 constant_dynamic-slice_fusion.4
  44.6 0.0 copy-done.5
  44.7 53.7 %all_gather.12 = bf16[16,32,256]{2,1,0:T(8,128)(2,1)S(1)} all-gather(bf16[1,32,256]{2,1,0:T(8,128)(2,1)S(1)} %copy-done.5), channel_id=1, replica_groups=mesh['ka'=16,'pts'=16] {'ka'}, dimensions={0}, use_global_device_ids=true | all-gather | bytes 278528 | tf_op jit(solution)/shard_map/all_gather | solution.py:39
  98.4 0.1 copy.20
  98.5 0.1 copy.13
  98.7 0.1 copy.19
  98.8 0.1 copy.10
  98.9 0.1 copy.21
  99.0 0.1 copy.16
  99.2 0.0 copy-done.3
  99.2 50.3 %all_gather.13 = bf16[16,32,256]{2,1,0:T(8,128)(2,1)S(1)} all-gather(bf16[1,32,256]{2,1,0:T(8,128)(2,1)S(1)} %copy-done.3), channel_id=1, replica_groups=mesh['ka'=16,'pts'=16] {'ka'}, dimensions={0}, use_global_device_ids=true | all-gather | bytes 278528 | tf_op jit(solution)/shard_map/all_gather | solution.py:38
  149.5 0.2 fusion.13
  149.7 0.2 fusion.12
  149.8 0.2 fusion.14
  150.0 171.3 %all-reduce.3.cloned.1.call-done = (bf16[256,4096]{1,0:T(8,128)(2,1)}, bf16[256,4096]{1,0:T(8,128)(2,1)}, bf16[256,4096]{1,0:T(8,128)(2,1)}) async-done(((bf16[256,4096]{1,0:T(8,128)(2,1)}, bf16[256,4096]{1,0:T(8,128)(2,1)}, bf16[256,4096]{1,0:T(8,128)(2,1)}), (bf16[256,4096]{1,0:T(8,128)(2,1)}, bf16[256,4096]{1,0:T(8,128)(2,1)}, bf16[256,4096]{1,0:T(8,128)(2,1)})) %all-reduce.3.cloned.1.call-update) | async-done | bytes 6291472 | tf_op jit(solution)/shard_map/psum | solution.py:9
  321.3 0.0 copy-start.1
  321.3 4.2 mul.44
  325.5 0.0 copy-start
  325.5 0.0 copy-done.1
  325.5 2.4 mul.40
  328.0 0.0 copy-start.2
  328.0 0.0 copy-done
  328.0 2.5 mul.48
  330.4 69.2 %all-gather.2.cloned.1.call-done = bf16[16,32,4096]{2,1,0:T(8,128)(2,1)} async-done(((bf16[1,32,4096]{2,1,0:T(8,128)(2,1)}), bf16[16,32,4096]{2,1,0:T(8,128)(2,1)}) %all-gather.2.cloned.1.call-update) | async-done | bytes 4194320 | tf_op jit(solution)/shard_map/all_gather | solution.py:37
  399.7 0.0 copy-done.2
  399.7 11.6 %fusion = bf16[8,256,32]{1,2,0:T(8,128)(2,1)S(1)} fusion(f32[256,4096]{1,0:T(8,128)} %mul.40, bf16[1,32,4096]{2,1,0:T(8,128)(2,1)S(1)} %copy-done.2, bf16[16,32,4096]{2,1,0:T(8,128)(2,1)} %all-gather.2.cloned.1.call-done, s32[]{:T(128)S(6)} %select_n.45, bf16[8,256,32]{1,0,2:T(8,128)(2,1)S(1)} %fusion.12), kind=kOutput, calls=%fused_computation.3 | convolution fusion | flops 1090519040 | bytes 4980740 | tf_op jit(solution)/shard_map/tmn,wn->tmw/dot_general | solution.py:21
  411.3 0.1 fusion.41
  411.5 11.8 %fusion.3 = bf16[8,256,32]{1,2,0:T(8,128)(2,1)S(1)} fusion(f32[256,4096]{1,0:T(8,128)} %mul.44, bf16[1,32,4096]{2,1,0:T(8,128)(2,1)S(1)} %copy-done.2, bf16[16,32,4096]{2,1,0:T(8,128)(2,1)} %all-gather.2.cloned.1.call-done, s32[]{:T(128)S(6)} %select_n.48, bf16[8,256,32]{1,0,2:T(8,128)(2,1)S(1)} %fusion.13), kind=kOutput, calls=%fused_computation.5 | convolution fusion | flops 1090519040 | bytes 4980740 | tf_op jit(solution)/shard_map/tmn,wn->tmw/dot_general | solution.py:21
  423.3 0.2 convolution_add_fusion.1
  423.5 11.6 %fusion.6 = bf16[8,256,32]{1,2,0:T(8,128)(2,1)S(1)} fusion(f32[256,4096]{1,0:T(8,128)} %mul.48, bf16[1,32,4096]{2,1,0:T(8,128)(2,1)S(1)} %copy-done.2, bf16[16,32,4096]{2,1,0:T(8,128)(2,1)} %all-gather.2.cloned.1.call-done, s32[]{:T(128)S(6)} %select_n.51, bf16[8,256,32]{1,0,2:T(8,128)(2,1)S(1)} %fusion.14), kind=kOutput, calls=%fused_computation.7 | convolution fusion | flops 1090519040 | bytes 4980740 | tf_op jit(solution)/shard_map/tmn,wn->tmw/dot_general | solution.py:21
  435.2 0.2 fusion.15
  435.3 0.8 copy.18
  436.1 0.0 reduce-scatter.2.cloned.1.call-update
  436.1 64.2 %reduce-scatter.2.cloned.1.call-done = f32[32,16]{0,1:T(8,128)} async-done(((f32[32,256]{0,1:T(8,128)}), f32[32,16]{0,1:T(8,128)}) %reduce-scatter.2.cloned.1.call-update) | async-done | bytes 2064 | tf_op jit(solution)/shard_map/reduce_scatter | solution.py:49
  (1 shorter events, 0.0 us)
Async XLA Ops:
  6.5 314.8 %all-reduce.3.cloned.1.call-start = ((), (), s32[]{:S(2)}) async-start(), calls=%async_computation.3 | async-start | bytes 12582912 | tf_op jit(solution)/shard_map/psum | solution.py:9
  14.1 0.7 copy-start.4
  14.1 23.8 %copy-start.6 = (s32[3,16]{1,0:T(4,128)S(1)}, s32[3,16]{1,0:T(4,128)}, u32[]{:S(2)}) copy-start(s32[3,16]{1,0:T(4,128)} %param.10) | copy-start | bytes 580
  14.1 30.6 %copy-start.5 = (bf16[1,32,256]{2,1,0:T(8,128)(2,1)S(1)}, bf16[1,32,256]{2,1,0:T(8,128)(2,1)}, u32[]{:S(2)}) copy-start(bf16[1,32,256]{2,1,0:T(8,128)(2,1)} %param.8) | copy-start | bytes 49156
  14.1 85.1 %copy-start.3 = (bf16[1,32,256]{2,1,0:T(8,128)(2,1)S(1)}, bf16[1,32,256]{2,1,0:T(8,128)(2,1)}, u32[]{:S(2)}) copy-start(bf16[1,32,256]{2,1,0:T(8,128)(2,1)} %param.7) | copy-start | bytes 49156
  14.1 385.5 %all-gather.2.cloned.1.call-start = ((), (), s32[]{:S(2)}) async-start(), calls=%async_computation.1 | async-start | bytes 4456448 | tf_op jit(solution)/shard_map/all_gather | solution.py:37
  37.8 462.5 %reduce-scatter.2.cloned.1.call-start = ((), (), s32[]{:S(2)}) async-start(), calls=%async_computation.2 | async-start | bytes 139264 | tf_op jit(solution)/shard_map/reduce_scatter | solution.py:49
  321.3 4.2 copy-start.1
  325.5 2.4 copy-start
  328.0 71.7 %copy-start.2 = (bf16[1,32,4096]{2,1,0:T(8,128)(2,1)S(1)}, bf16[1,32,4096]{2,1,0:T(8,128)(2,1)}, u32[]{:S(2)}) copy-start(bf16[1,32,4096]{2,1,0:T(8,128)(2,1)} %all_gather.14) | copy-start | bytes 786436
Sparse Core Ops, SparseCore 0:
  14.2 307.0 all-reduce.2
  323.8 75.8 all-gather.1
  436.2 64.0 reduce-scatter.1
where the time goes:
time: 507 us
  waiting for transfers between devices  305 us (60%)
  blocking collectives  127 us (25%)
  matrix products  36.1 us (7%)
  between operations  21.2 us (4%)
  other arithmetic  13.5 us (3%)
    psum x1, waiting for transfers between devices, broadcast(): return lax.psum(jnp.where(mine, shard, jnp.zeros_like(shard)), axis)  171 us
    all_gather x1, waiting for transfers between devices, shards(): lax.all_gather(own_full, 'ka', axis=0, tiled=True)  69.2 us
    reduce_scatter x1, waiting for transfers between devices, shards(): lax.psum_scatter(term, 'pts', scatter_dimension=1, tiled=True)  64.2 us
    all_gather x1, blocking collectives, shards(): lax.all_gather(trials, 'ka', axis=0, tiled=True)  53.7 us
    all_gather x1, blocking collectives, shards(): lax.all_gather(conduction, 'ka', axis=0, tiled=True)  50.3 us
    dot_general x3, matrix products, kernel_term(): jnp.einsum('tmn,wn->tmw', weighted, own_full, preferred_element_type=jnp....  35.1 us
    all_gather x1, blocking collectives, shards(): own_full = lax.all_gather(valence, 'pts', axis=2, tiled=True)  23 us
    mul x4, other arithmetic, kernel_term(): weighted = (panel.astype(jnp.float32)[None] * image).astype(jnp.bfloat16)  13.5 us
  transfers between devices with their start and end apart: 3, of which 3 were waited for; matrix products, arithmetic and copies ran while one was open for 2% of the time, Pallas kernels for 0%

commit v1 on v0

v1 whole, which is shorter than its diff:
```python
import jax
import jax.numpy as jnp
from jax import lax
from jax.experimental import pallas as pl
from jax.experimental.pallas import tpu as pltpu
from jax.sharding import PartitionSpec as P


F32 = jnp.float32
BF16 = jnp.bfloat16
AXES = ("ka", "pts")


def coords(i):
    return [i // 64, (i // 16) % 4, (i // 8) % 2, (i // 2) % 4, i % 2]


def linear(v):
    return (((v[0] * 4 + v[1]) * 2 + v[2]) * 4 + v[3]) * 2 + v[4]


def move(a, f):
    pairs = []
    for i in range(256):
        v = coords(i)
        pairs.append((i, linear(f(v))))
    return lax.ppermute(a, AXES, pairs)


def flip(a, dim, mask):
    def f(v):
        w = list(v)
        w[dim] ^= mask if dim in (2, 4) or v[4] == 0 else 4 - mask
        return w

    return move(a, f)


def gray(s):
    return s ^ (s >> 1)


def half_pos(s):
    return 2 * ((s ^ (s >> 1)) & 1) + (s >> 1)


def pos_gather(s, c):
    return jnp.where(c == 0, gray(s), half_pos(s))


def pos_reduce(s, c):
    return jnp.where(c == 0, half_pos(s), gray(s))


def double(a, dim, mask):
    return jnp.concatenate([a, flip(a, dim, mask)], axis=0)


def cut_kernel(meta, w, o0, o1, o2, o3, sems):
    x = meta[0]
    copies = []
    for d, o in enumerate((o0, o1, o2, o3)):
        at = (x + d) & 3
        for zs in range(2):
            src = w.at[0, :, pl.ds(pl.multiple_of(zs * 2048 + at * 512, 512), 512)]
            dst = o.at[:, zs * 512 : zs * 512 + 512]
            copies.append(pltpu.make_async_copy(src, dst, sems.at[d * 2 + zs]))
    for cp in copies:
        cp.start()
    for cp in copies:
        cp.wait()


def cut(meta, w):
    hbm = pl.BlockSpec(memory_space=pl.ANY)
    vm = pl.BlockSpec(memory_space=pltpu.VMEM)
    return pl.pallas_call(
        cut_kernel,
        out_shape=[jax.ShapeDtypeStruct((256, 1024), BF16)] * 4,
        in_specs=[pl.BlockSpec(memory_space=pltpu.SMEM), hbm],
        out_specs=[vm] * 4,
        scratch_shapes=[pltpu.SemaphoreType.DMA((8,))],
        name="cut",
    )(meta, w)


def kernel(meta, w0, w1, w2, w3, va, vb, ct, out, send, vf, blk, back, da, db, ga, gb, wt):
    x, zh, zl, y, c = meta[0], meta[1], meta[2], meta[3], meta[4]

    def place(k, own, far):
        kx, kz = k // 4, k % 4
        py = pos_gather(kx ^ y, c)
        pz = pos_gather(kz ^ zh, c)
        far_py = pos_gather(kx ^ y, 1 - c)
        far_pz = pos_gather(kz ^ zh, 1 - c)
        for zs in range(2):
            rz = zs ^ zl
            here = (py * 2 + rz) * 4 + pz
            there = (far_py * 2 + rz) * 4 + far_pz
            for cs in range(2):
                src = (own, far)[cs]
                yield zs, cs, src, jnp.where(c == cs, here, there)

    def spread(first, second):
        def body(k, _):
            for zs, cs, src, idx in place(k, first, second):
                col = (zs * 2 + cs) * 256
                vf[k, :, col : col + 256] = src[idx].astype(F32)
            return 0

        lax.fori_loop(0, 16, body, 0)

    def slot_active(q):
        return (meta[8 + q] % 4) == zh

    any_active = slot_active(0) | slot_active(1) | slot_active(2)

    back[...] = jnp.zeros_like(back)

    @pl.when(any_active)
    def _():
        pl.when(c == 0)(lambda: spread(va, vb))
        pl.when(c == 1)(lambda: spread(vb, va))

        lane = lax.broadcasted_iota(jnp.int32, (32, 8, 256), 2)
        row = lax.broadcasted_iota(jnp.int32, (32, 8, 256), 1)
        same = (lane & 7) == row

        def blocks(k, _):
            kx, kz = k // 4, k % 4
            idx = pos_gather(kz ^ zh, c) * 9 + pos_gather(kx ^ x, c) * 2
            cond = ct[idx].astype(F32)
            tri = ct[idx + 1].astype(F32)
            lhs = jnp.where(same, tri[:, None, :], 0.0).reshape(256, 256).astype(BF16)
            rhs = jnp.broadcast_to(cond[:, None, :], (32, 8, 256)).reshape(256, 256).astype(BF16)
            got = lax.dot_general(lhs, rhs, (((1,), (0,)), ((), ())), preferred_element_type=F32)
            blk[k] = got.astype(BF16).astype(F32)
            return 0

        lax.fori_loop(0, 16, blocks, 0)

    def build(dref, k, p, g):
        own = vf[k]
        for i in range(16):
            line = vf[p, pl.ds(g * 16 + i, 1), :]
            dref[i * 32 : (i + 1) * 32, :] = (own * line).astype(BF16)

    def multiply(gref, dref):
        gref[...] = lax.dot_general(
            dref[...], wt[...], (((1,), (0,)), ((), ())), preferred_element_type=F32
        )

    def contract(gref, k, p, g):
        for s in range(4):
            acc = [back[k, t * 32 + s * 8 : t * 32 + s * 8 + 8, :] for t in range(8)]
            for i in range(16):
                val = gref[i * 32 + s * 8 : i * 32 + s * 8 + 8, :]
                for t in range(8):
                    acc[t] = acc[t] + blk[p, (g * 16 + i) * 8 + t : (g * 16 + i) * 8 + t + 1, :] * val
            for t in range(8):
                back[k, t * 32 + s * 8 : t * 32 + s * 8 + 8, :] = acc[t]

    def one(q, _):
        @pl.when(slot_active(q))
        def _():
            d = (x - meta[8 + q] // 4) & 3
            for j, w in enumerate((w0, w1, w2, w3)):

                def turn(w=w):
                    wt[...] = w[...].T

                pl.when(d == j)(turn)
            db[...] = jnp.zeros_like(db)
            ga[...] = jnp.zeros_like(ga)

            def body(k, _):
                kc = jnp.minimum(k, 15)
                pc = meta[16 + q * 16 + kc]
                ko = jnp.maximum(k - 1, 0)
                po = meta[16 + q * 16 + ko]
                multiply(gb, db)
                build(da, kc, pc, 0)
                contract(ga, ko, po, 0)
                multiply(ga, da)
                build(db, kc, pc, 1)
                contract(gb, ko, po, 1)
                return 0

            lax.fori_loop(0, 17, body, 0)

        return 0

    lax.fori_loop(0, 3, one, 0)

    r = lax.broadcasted_iota(jnp.int32, (32, 32), 0)
    col = lax.broadcasted_iota(jnp.int32, (32, 32), 1)
    ry = (r >> 2) & 3
    even = jnp.where(ry == 0, 0, jnp.where(ry == 1, 3, ry - 1))
    ys = jnp.where(((r >> 4) ^ c) == 0, even, ry ^ (ry >> 1))
    want = ((((r >> 1) & 1) ^ zl) * 4 + (ys ^ y)) * 4 + ((r >> 4) ^ c) * 2 + (r & 1)
    pick = jnp.where(col == want, 1.0, 0.0).astype(BF16)

    def last(k, _):
        kx, kz = k // 4, k % 4
        idx = pos_gather(kz ^ zh, c) * 9 + pos_gather(kx ^ x, c) * 2
        cond = lax.dot_general(
            pick, ct[idx], (((1,), (0,)), ((), ())), preferred_element_type=F32
        ).astype(BF16)
        b = back[k]
        hi = b.astype(BF16)
        lo = (b - hi.astype(F32)).astype(BF16)
        nt = (((1,), (1,)), ((), ()))
        res = lax.dot_general(cond, hi, nt, preferred_element_type=F32)
        res = res + lax.dot_general(cond, lo, nt, preferred_element_type=F32)
        at = pos_reduce(kx ^ x, c) * 4 + pos_reduce(kz ^ zh, c)
        out[at] = res[:16]
        far = pos_reduce(kx ^ x, 1 - c) * 4 + pos_reduce(kz ^ zh, 1 - c)
        send[far] = res[16:].astype(BF16)
        return 0

    lax.fori_loop(0, 16, last, 0)


def local(meta, w0, w1, w2, w3, va, vb, ct):
    vm = pl.BlockSpec(memory_space=pltpu.VMEM)
    return pl.pallas_call(
        kernel,
        out_shape=[
            jax.ShapeDtypeStruct((16, 16, 256), F32),
            jax.ShapeDtypeStruct((16, 16, 256), BF16),
        ],
        in_specs=[pl.BlockSpec(memory_space=pltpu.SMEM)] + [vm] * 7,
        out_specs=[vm, vm],
        scratch_shapes=[
            pltpu.VMEM((16, 32, 1024), F32),
            pltpu.VMEM((16, 256, 256), F32),
            pltpu.VMEM((16, 256, 256), F32),
            pltpu.VMEM((512, 1024), BF16),
            pltpu.VMEM((512, 1024), BF16),
            pltpu.VMEM((512, 256), F32),
            pltpu.VMEM((512, 256), F32),
            pltpu.VMEM((1024, 256), BF16),
        ],
        compiler_params=pltpu.CompilerParams(vmem_limit_bytes=48 << 20),
        name="screened",
    )(meta, w0, w1, w2, w3, va, vb, ct)


def steps(valence, conduction, trials, w_panels, partner, owner):
    ka = lax.axis_index("ka")
    pts = lax.axis_index("pts")
    x, zh = ka // 4, ka % 4
    zl, y, c = pts // 8, (pts // 2) % 4, pts % 2
    spot = jnp.arange(16, dtype=jnp.int32)
    place = jnp.where(spot == 0, x, jnp.where(spot == 1, zh, jnp.where(spot == 2, zl, jnp.where(spot == 3, y, c))))
    place = place.astype(jnp.int32)
    meta = jnp.concatenate([place[:8], owner, place[11:], partner.reshape(-1)])

    got = list(cut(place, w_panels))
    for d in (1, 2, 3):

        def shift(v, d=d):
            return [(v[0] + d) % 4] + v[1:]

        got[d] = move(got[d], shift)

    ct = jnp.stack([conduction[0], trials[0]])[None]
    ct = double(ct, 0, 1)

    def swap(v):
        return [v[3], v[1], v[2], v[0], v[4]]

    va = move(valence, swap)

    ct = double(ct, 0, 3)
    ct = jnp.concatenate([ct.reshape(8, 32, 256), va], axis=0)
    ct = double(ct, 1, 1)
    ct = double(ct, 1, 3)
    va = ct[8::9]
    va = double(va, 2, 1)
    va = double(va, 3, 1)
    va = double(va, 3, 3)
    vb = flip(va, 4, 1)

    part, send = local(meta, *got, va, vb, ct)

    part = part + flip(send, 4, 1).astype(F32)
    part = part[:, :8] + flip(part[:, 8:].astype(BF16), 3, 1).astype(F32)
    part = part[:, :4] + flip(part[:, 4:].astype(BF16), 3, 3).astype(F32)
    part = part[:8] + flip(part[8:], 0, 1)
    part = part[:4] + flip(part[4:], 0, 3)
    part = part[:, :2] + flip(part[:, 2:], 2, 1)
    part = part[:2] + flip(part[2:], 1, 1)
    part = part[:1] + flip(part[1:], 1, 3)
    return part.reshape(2, 8, 32).transpose(2, 0, 1).reshape(1, 32, 16)


def solution(mesh):
    placed = (
        P("ka", None, "pts"),
        P("ka", None, "pts"),
        P("ka", None, None),
        P("ka", "pts", None),
        P(),
        P(),
    )
    return jax.shard_map(
        steps, mesh=mesh, in_specs=placed, out_specs=P("ka", None, "pts"), check_vma=False
    )
```

time: 507 us -> 169 us (0.33)
  waiting for transfers between devices: 305 us -> 63.6 us
  blocking collectives: 127 us -> 0 us
  Pallas kernels: 0 us -> 59.8 us
  starting transfers between devices: 0.09 us -> 39 us
  matrix products: 36.1 us -> 0 us
  between operations: 21.2 us -> 0.21 us
  other arithmetic: 13.5 us -> 1.65 us
    psum x1 -> x0, waiting for transfers between devices: 171 us -> none  [broadcast(): return lax.psum(jnp.where(mine, shard, jnp.zeros_like(shard)), axis)]
    all_gather x3 -> x0, blocking collectives: 127 us -> none  [the longest x1 53.7 us: shards(): lax.all_gather(trials, 'ka', axis=0, tiled=True)]
    all_gather x1 -> x0, waiting for transfers between devices: 69.2 us -> none  [shards(): lax.all_gather(own_full, 'ka', axis=0, tiled=True)]
    reduce_scatter x1 -> x0, waiting for transfers between devices: 64.2 us -> none  [shards(): lax.psum_scatter(term, 'pts', scatter_dimension=1, tiled=True)]
    ppermute x0 -> x20, waiting for transfers between devices: none -> 63.6 us  [move(): return lax.ppermute(a, AXES, pairs)]
    pallas_call x0 -> x2, Pallas kernels: none -> 59.8 us  [the longest x1 56.2 us: local(): pl.pallas_call(kernel, out_shape=[jax.ShapeDtypeStruct((16, 16, 256), F32...]
    ppermute x0 -> x20, starting transfers between devices: none -> 39 us  [move(): return lax.ppermute(a, AXES, pairs)]
    dot_general x9 -> x0, matrix products: 36.1 us -> none  [the longest x3 35.1 us: kernel_term(): jnp.einsum('tmn,wn->tmw', weighted, own_full, preferred_element_type=jnp....]
  transfers between devices with their start and end apart: 3 -> 20, of which waited for: 3 -> 16; matrix products, arithmetic and copies ran while one was open for 2% -> 0% of each run, Pallas kernels for 0% -> 2%
where the time goes in v1:
time: 169 us; the launch traced here: 166 us
  waiting for transfers between devices  63.6 us (38%)
  Pallas kernels  59.8 us (35%)
  starting transfers between devices  39 us (23%)
  local copies, waits for them, and re-layouts  1.95 us (1%)
    ppermute x20, waiting for transfers between devices, move(): return lax.ppermute(a, AXES, pairs)  63.6 us
    pallas_call x1, Pallas kernels, local(): pl.pallas_call(kernel, out_shape=[jax.ShapeDtypeStruct((16, 16, 256), F32...  56.2 us
    ppermute x20, starting transfers between devices, move(): return lax.ppermute(a, AXES, pairs)  39 us
    pallas_call x1, Pallas kernels, cut(): pl.pallas_call(cut_kernel, out_shape=[jax.ShapeDtypeStruct((256, 1024), B...  3.69 us
  transfers between devices with their start and end apart: 20, of which 16 were waited for; matrix products, arithmetic and copies ran while one was open for 0% of the time, Pallas kernels for 2%

profile of v1, /device:TPU:2, one launch (start us, length us, event | category | flops | bytes accessed | tf_op | source)
XLA Modules:
  0.0 166.2 jit_solution(8512162483698592363)
XLA Ops:
  0.0 0.7 maximum_bitcast_fusion
  0.7 2.2 %collective-permute-start.3 = (bf16[1,2,32,256]{3,2,1,0:T(8,128)(2,1)S(1)}, bf16[1,2,32,256]{3,2,1,0:T(8,128)(2,1)S(1)}, u32[]{:S(2)}, u32[]{:S(2)}) collective-permute-start(bf16[1,2,32,256]{3,2,1,0:T(8,128)(2,1)S(1)} %maximum_bitcast_fusion), channel_id=1, source_target_pairs={{0,64},{1,193},{2,66},{3,195},{4,68},{5,197},{6,70},{7,199},{8,72}... | collective-permute-start | bytes 98312 | tf_op jit(solution)/shard_map/ppermute | solution.py:27
  3.0 1.9 %collective-permute-done.3 = bf16[1,2,32,256]{3,2,1,0:T(8,128)(2,1)S(1)} collective-permute-done((bf16[1,2,32,256]{3,2,1,0:T(8,128)(2,1)S(1)}, bf16[1,2,32,256]{3,2,1,0:T(8,128)(2,1)S(1)}, u32[]{:S(2)}, u32[]{:S(2)}) %collective-permute-start.3) | collective-permute-done | bytes 32800 | tf_op jit(solution)/shard_map/ppermute | solution.py:27
  4.9 1.4 collective-permute-start.4
  6.2 4.7 %collective-permute-start.5 = (bf16[1,32,256]{2,1,0:T(8,128)(2,1)}, bf16[1,32,256]{2,1,0:T(8,128)(2,1)S(1)}, u32[]{:S(2)}, u32[]{:S(2)}) collective-permute-start(bf16[1,32,256]{2,1,0:T(8,128)(2,1)} %param.6), channel_id=1, source_target_pairs={{0,0},{1,1},{2,64},{3,65},{4,128},{5,129},{6,192},{7,193},{8,8},{9... | collective-permute-start | bytes 49160 | tf_op jit(solution)/shard_map/ppermute | solution.py:27
  11.0 0.0 collective-permute-done.4
  11.0 2.0 %collective-permute-done.5 = bf16[1,32,256]{2,1,0:T(8,128)(2,1)S(1)} collective-permute-done((bf16[1,32,256]{2,1,0:T(8,128)(2,1)}, bf16[1,32,256]{2,1,0:T(8,128)(2,1)S(1)}, u32[]{:S(2)}, u32[]{:S(2)}) %collective-permute-start.5) | collective-permute-done | bytes 16416 | tf_op jit(solution)/shard_map/ppermute | solution.py:27
  13.0 3.4 %collective-permute-start.6 = (bf16[9,32,256]{2,1,0:T(8,128)(2,1)S(1)}, bf16[9,32,256]{2,1,0:T(8,128)(2,1)S(1)}, u32[]{:S(2)}, u32[]{:S(2)}) collective-permute-start(bf16[9,32,256]{2,1,0:T(8,128)(2,1)S(1)} %pad_maximum_fusion.4), channel_id=1, source_target_pairs={{0,16},{1,49},{2,18},{3,51},{4,20},{5,53},{6,22},{7,55},{8,24},{9,... | collective-permute-start | bytes 442376 | tf_op jit(solution)/shard_map/ppermute | solution.py:27
  16.4 3.7 %collective-permute-done.6 = bf16[9,32,256]{2,1,0:T(8,128)(2,1)S(1)} collective-permute-done((bf16[9,32,256]{2,1,0:T(8,128)(2,1)S(1)}, bf16[9,32,256]{2,1,0:T(8,128)(2,1)S(1)}, u32[]{:S(2)}, u32[]{:S(2)}) %collective-permute-start.6) | collective-permute-done | bytes 147488 | tf_op jit(solution)/shard_map/ppermute | solution.py:27
  20.1 6.6 %collective-permute-start.7 = (bf16[18,32,256]{2,1,0:T(8,128)(2,1)S(1)}, bf16[18,32,256]{2,1,0:T(8,128)(2,1)S(1)}, u32[]{:S(2)}, u32[]{:S(2)}) collective-permute-start(bf16[18,32,256]{2,1,0:T(8,128)(2,1)S(1)} %pad_maximum_fusion.2), channel_id=1, source_target_pairs={{0,48},{1,17},{2,50},{3,19},{4,52},{5,21},{6,54},{7,23},{8,56},{9,... | collective-permute-start | bytes 884744 | tf_op jit(solution)/shard_map/ppermute | solution.py:27
  26.7 7.4 %collective-permute-done.7 = bf16[18,32,256]{2,1,0:T(8,128)(2,1)S(1)} collective-permute-done((bf16[18,32,256]{2,1,0:T(8,128)(2,1)S(1)}, bf16[18,32,256]{2,1,0:T(8,128)(2,1)S(1)}, u32[]{:S(2)}, u32[]{:S(2)}) %collective-permute-start.7) | collective-permute-done | bytes 294944 | tf_op jit(solution)/shard_map/ppermute | solution.py:27
  34.1 0.1 pad_maximum_fusion.ct
  34.1 0.0 copy-start.2
  34.1 0.0 copy-start.3
  34.2 0.7 collective-permute-start.8
  34.8 3.7 %collective-permute-done.8 = bf16[4,32,256]{2,1,0:T(8,128)(2,1)S(1)} collective-permute-done((bf16[4,32,256]{2,1,0:T(8,128)(2,1)S(1)}, bf16[4,32,256]{2,1,0:T(8,128)(2,1)S(1)}, u32[]{:S(2)}, u32[]{:S(2)}) %collective-permute-start.8) | collective-permute-done | bytes 65568 | tf_op jit(solution)/shard_map/ppermute | solution.py:27
  38.5 0.1 collective-permute-start.9
  38.6 5.0 %collective-permute-done.9 = bf16[8,32,256]{2,1,0:T(8,128)(2,1)S(1)} collective-permute-done((bf16[8,32,256]{2,1,0:T(8,128)(2,1)S(1)}, bf16[8,32,256]{2,1,0:T(8,128)(2,1)S(1)}, u32[]{:S(2)}, u32[]{:S(2)}) %collective-permute-start.9) | collective-permute-done | bytes 131104 | tf_op jit(solution)/shard_map/ppermute | solution.py:27
  43.6 7.5 %collective-permute-start.10 = (bf16[16,32,256]{2,1,0:T(8,128)(2,1)S(1)}, bf16[16,32,256]{2,1,0:T(8,128)(2,1)S(1)}, u32[]{:S(2)}, u32[]{:S(2)}) collective-permute-start(bf16[16,32,256]{2,1,0:T(8,128)(2,1)S(1)} %pad_maximum_fusion.3), channel_id=1, source_target_pairs={{0,6},{1,3},{2,4},{3,1},{4,2},{5,7},{6,0},{7,5},{8,14},{9,11},{10,... | collective-permute-start | bytes 786440 | tf_op jit(solution)/shard_map/ppermute | solution.py:27
  51.1 0.5 compare_select_fusion.3.meta
  51.6 0.0 copy-start.1
  51.6 3.7 %cut.1 = (bf16[256,1024]{1,0:T(8,128)(2,1)}, bf16[256,1024]{1,0:T(8,128)(2,1)}, bf16[256,1024]{1,0:T(8,128)(2,1)}, bf16[256,1024]{1,0:T(8,128)(2,1)}) custom-call(s32[16]{0:T(128)} %compare_select_fusion.3.meta, bf16[1,256,4096]{2,1,0:T(8,128)(2,1)} %w.1), custom_call_target="tpu_custom_call" | custom-call | tf_op jit(solution)/shard_map/cut/pallas_call | solution.py:77
  55.4 0.1 collective-permute-start
  55.4 5.2 %collective-permute-start.1 = (bf16[256,1024]{1,0:T(8,128)(2,1)}, bf16[256,1024]{1,0:T(8,128)(2,1)S(1)}, u32[]{:S(2)}, u32[]{:S(2)}) collective-permute-start(bf16[256,1024]{1,0:T(8,128)(2,1)} %get-tuple-element.13), channel_id=1, source_target_pairs={{0,128},{1,129},{2,130},{3,131},{4,132},{5,133},{6,134},{7,135},{8... | collective-permute-start | bytes 1572872 | tf_op jit(solution)/shard_map/ppermute | solution.py:27
  60.6 0.0 collective-permute-start.2
  60.6 0.0 collective-permute-done.10
  60.6 0.1 pad_maximum_fusion.1.va
  60.7 0.1 collective-permute-start.11
  60.8 0.0 copy-done.1
  60.8 0.1 slice.54
  60.9 0.0 copy-done.2
  60.9 0.1 reshape.12
  61.0 0.0 copy-done.3
  61.0 0.1 pad_add_fusion.meta
  61.1 10.4 %collective-permute-done.w1 = bf16[256,1024]{1,0:T(8,128)(2,1)S(1)} collective-permute-done((bf16[256,1024]{1,0:T(8,128)(2,1)}, bf16[256,1024]{1,0:T(8,128)(2,1)S(1)}, u32[]{:S(2)}, u32[]{:S(2)}) %collective-permute-start) | collective-permute-done | bytes 524320 | tf_op jit(solution)/shard_map/ppermute | solution.py:27
  71.4 0.0 collective-permute-done.1.w2
  71.4 3.2 %collective-permute-done.2.w3 = bf16[256,1024]{1,0:T(8,128)(2,1)S(1)} collective-permute-done((bf16[256,1024]{1,0:T(8,128)(2,1)}, bf16[256,1024]{1,0:T(8,128)(2,1)S(1)}, u32[]{:S(2)}, u32[]{:S(2)}) %collective-permute-start.2) | collective-permute-done | bytes 524320 | tf_op jit(solution)/shard_map/ppermute | solution.py:27
  74.6 0.0 collective-permute-done.11.vb
  74.6 0.0 copy-start
  74.6 1.0 copy-done
  75.7 56.2 %screened.1 = (f32[16,16,256]{2,1,0:T(8,128)S(1)}, bf16[16,16,256]{2,1,0:T(8,128)(2,1)S(1)}) custom-call(s32[64]{0:T(128)S(1)} %pad_add_fusion.meta, bf16[256,1024]{1,0:T(8,128)(2,1)S(1)} %copy-done, bf16[256,1024]{1,0:T(8,128)(2,1)S(1)} %collective-permute-done.w1, bf16[256,1024]{1,0:T(8,128)(2,1)S(1)} %collective-permute-done.1.w2, ...), custom_call_target="tpu_custom_call" | custom-call | tf_op jit(solution)/shard_map/screened/pallas_call | solution.py:226
  131.8 0.0 collective-permute-start.12
  131.9 1.3 collective-permute-done.12
  133.3 0.8 collective-permute-start.13
  134.1 3.5 %collective-permute-done.13 = bf16[16,8,256]{2,1,0:T(8,128)(2,1)S(1)} collective-permute-done((bf16[16,8,256]{2,1,0:T(8,128)(2,1)S(1)}, bf16[16,8,256]{2,1,0:T(8,128)(2,1)S(1)}, u32[]{:S(2)}, u32[]{:S(2)}) %collective-permute-start.13) | collective-permute-done | bytes 65568 | tf_op jit(solution)/shard_map/ppermute | solution.py:27
  137.7 1.1 collective-permute-start.14
  138.7 4.2 %collective-permute-done.14 = bf16[16,4,256]{2,1,0:T(4,128)(2,1)S(1)} collective-permute-done((bf16[16,4,256]{2,1,0:T(4,128)(2,1)S(1)}, bf16[16,4,256]{2,1,0:T(4,128)(2,1)S(1)}, u32[]{:S(2)}, u32[]{:S(2)}) %collective-permute-start.14) | collective-permute-done | bytes 32800 | tf_op jit(solution)/shard_map/ppermute | solution.py:27
  142.9 2.8 %collective-permute-start.15 = (f32[8,4,256]{2,1,0:T(4,128)S(1)}, f32[8,4,256]{2,1,0:T(4,128)S(1)}, u32[]{:S(2)}, u32[]{:S(2)}) collective-permute-start(f32[8,4,256]{2,1,0:T(4,128)S(1)} %slice.75), channel_id=1, source_target_pairs={{0,64},{1,193},{2,66},{3,195},{4,68},{5,197},{6,70},{7,199},{8,72}... | collective-permute-start | bytes 98312 | tf_op jit(solution)/shard_map/ppermute | solution.py:27
  145.7 1.9 %collective-permute-done.15 = f32[8,4,256]{2,1,0:T(4,128)S(1)} collective-permute-done((f32[8,4,256]{2,1,0:T(4,128)S(1)}, f32[8,4,256]{2,1,0:T(4,128)S(1)}, u32[]{:S(2)}, u32[]{:S(2)}) %collective-permute-start.15) | collective-permute-done | bytes 32800 | tf_op jit(solution)/shard_map/ppermute | solution.py:27
  147.7 0.4 collective-permute-start.16
  148.1 3.4 %collective-permute-done.16 = f32[4,4,256]{2,1,0:T(4,128)S(1)} collective-permute-done((f32[4,4,256]{2,1,0:T(4,128)S(1)}, f32[4,4,256]{2,1,0:T(4,128)S(1)}, u32[]{:S(2)}, u32[]{:S(2)}) %collective-permute-start.16) | collective-permute-done | bytes 16416 | tf_op jit(solution)/shard_map/ppermute | solution.py:27
  151.5 1.9 %collective-permute-start.17 = (f32[4,2,256]{2,1,0:T(2,128)S(1)}, f32[4,2,256]{2,1,0:T(2,128)S(1)}, u32[]{:S(2)}, u32[]{:S(2)}) collective-permute-start(f32[4,2,256]{2,1,0:T(2,128)S(1)} %slice.79), channel_id=1, source_target_pairs={{0,8},{1,9},{2,10},{3,11},{4,12},{5,13},{6,14},{7,15},{8,0},{9,1},... | collective-permute-start | bytes 24584 | tf_op jit(solution)/shard_map/ppermute | solution.py:27
  153.4 1.8 %collective-permute-done.17 = f32[4,2,256]{2,1,0:T(2,128)S(1)} collective-permute-done((f32[4,2,256]{2,1,0:T(2,128)S(1)}, f32[4,2,256]{2,1,0:T(2,128)S(1)}, u32[]{:S(2)}, u32[]{:S(2)}) %collective-permute-start.17) | collective-permute-done | bytes 8224 | tf_op jit(solution)/shard_map/ppermute | solution.py:27
  155.3 0.1 collective-permute-start.18
  155.4 4.5 %collective-permute-done.18 = f32[2,2,256]{2,1,0:T(2,128)S(1)} collective-permute-done((f32[2,2,256]{2,1,0:T(2,128)S(1)}, f32[2,2,256]{2,1,0:T(2,128)S(1)}, u32[]{:S(2)}, u32[]{:S(2)}) %collective-permute-start.18) | collective-permute-done | bytes 4128 | tf_op jit(solution)/shard_map/ppermute | solution.py:27
  159.9 0.0 collective-permute-start.19
  159.9 5.7 %collective-permute-done.19 = f32[1,2,256]{2,1,0:T(2,128)S(1)} collective-permute-done((f32[1,2,256]{2,1,0:T(2,128)S(1)}, f32[1,2,256]{2,1,0:T(2,128)S(1)}, u32[]{:S(2)}, u32[]{:S(2)}) %collective-permute-start.19) | collective-permute-done | bytes 2080 | tf_op jit(solution)/shard_map/ppermute | solution.py:27
  165.6 0.7 reshape.14
  (22 shorter events, 0.3 us)
Async XLA Ops:
  0.7 4.1 %collective-permute-start.3 = (bf16[1,2,32,256]{3,2,1,0:T(8,128)(2,1)S(1)}, bf16[1,2,32,256]{3,2,1,0:T(8,128)(2,1)S(1)}, u32[]{:S(2)}, u32[]{:S(2)}) collective-permute-start(bf16[1,2,32,256]{3,2,1,0:T(8,128)(2,1)S(1)} %maximum_bitcast_fusion), channel_id=1, source_target_pairs={{0,64},{1,193},{2,66},{3,195},{4,68},{5,197},{6,70},{7,199},{8,72}... | collective-permute-start | bytes 98312 | tf_op jit(solution)/shard_map/ppermute | solution.py:27
  4.9 6.1 %collective-permute-start.4 = (bf16[2,2,32,256]{3,2,1,0:T(8,128)(2,1)S(1)}, bf16[2,2,32,256]{3,2,1,0:T(8,128)(2,1)S(1)}, u32[]{:S(2)}, u32[]{:S(2)}) collective-permute-start(bf16[2,2,32,256]{3,2,1,0:T(8,128)(2,1)S(1)} %pad_maximum_fusion.7), channel_id=1, source_target_pairs={{0,192},{1,65},{2,194},{3,67},{4,196},{5,69},{6,198},{7,71},{8,200... | collective-permute-start | bytes 196616 | tf_op jit(solution)/shard_map/ppermute | solution.py:27
  6.2 6.7 %collective-permute-start.5 = (bf16[1,32,256]{2,1,0:T(8,128)(2,1)}, bf16[1,32,256]{2,1,0:T(8,128)(2,1)S(1)}, u32[]{:S(2)}, u32[]{:S(2)}) collective-permute-start(bf16[1,32,256]{2,1,0:T(8,128)(2,1)} %param.6), channel_id=1, source_target_pairs={{0,0},{1,1},{2,64},{3,65},{4,128},{5,129},{6,192},{7,193},{8,8},{9... | collective-permute-start | bytes 49160 | tf_op jit(solution)/shard_map/ppermute | solution.py:27
  13.0 7.1 %collective-permute-start.6 = (bf16[9,32,256]{2,1,0:T(8,128)(2,1)S(1)}, bf16[9,32,256]{2,1,0:T(8,128)(2,1)S(1)}, u32[]{:S(2)}, u32[]{:S(2)}) collective-permute-start(bf16[9,32,256]{2,1,0:T(8,128)(2,1)S(1)} %pad_maximum_fusion.4), channel_id=1, source_target_pairs={{0,16},{1,49},{2,18},{3,51},{4,20},{5,53},{6,22},{7,55},{8,24},{9,... | collective-permute-start | bytes 442376 | tf_op jit(solution)/shard_map/ppermute | solution.py:27
  20.1 13.9 %collective-permute-start.7 = (bf16[18,32,256]{2,1,0:T(8,128)(2,1)S(1)}, bf16[18,32,256]{2,1,0:T(8,128)(2,1)S(1)}, u32[]{:S(2)}, u32[]{:S(2)}) collective-permute-start(bf16[18,32,256]{2,1,0:T(8,128)(2,1)S(1)} %pad_maximum_fusion.2), channel_id=1, source_target_pairs={{0,48},{1,17},{2,50},{3,19},{4,52},{5,21},{6,54},{7,23},{8,56},{9,... | collective-permute-start | bytes 884744 | tf_op jit(solution)/shard_map/ppermute | solution.py:27
  34.1 26.8 %copy-start.2 = (s32[3,16]{1,0:T(4,128)S(1)}, s32[3,16]{1,0:T(4,128)}, u32[]{:S(2)}) copy-start(s32[3,16]{1,0:T(4,128)} %param.10) | copy-start | bytes 580
  34.1 26.8 %copy-start.3 = (s32[3]{0:T(128)S(1)}, s32[3]{0:T(128)}, u32[]{:S(2)}) copy-start(s32[3]{0:T(128)} %param.11) | copy-start | bytes 40
  34.2 4.4 %collective-permute-start.8 = (bf16[4,32,256]{2,1,0:T(8,128)(2,1)S(1)}, bf16[4,32,256]{2,1,0:T(8,128)(2,1)S(1)}, u32[]{:S(2)}, u32[]{:S(2)}) collective-permute-start(bf16[4,32,256]{2,1,0:T(8,128)(2,1)S(1)} %slice.55), channel_id=1, source_target_pairs={{0,8},{1,9},{2,10},{3,11},{4,12},{5,13},{6,14},{7,15},{8,0},{9,1},... | collective-permute-start | bytes 196616 | tf_op jit(solution)/shard_map/ppermute | solution.py:27
  38.5 5.1 %collective-permute-start.9 = (bf16[8,32,256]{2,1,0:T(8,128)(2,1)S(1)}, bf16[8,32,256]{2,1,0:T(8,128)(2,1)S(1)}, u32[]{:S(2)}, u32[]{:S(2)}) collective-permute-start(bf16[8,32,256]{2,1,0:T(8,128)(2,1)S(1)} %pad_maximum_fusion.6), channel_id=1, source_target_pairs={{0,2},{1,7},{2,0},{3,5},{4,6},{5,3},{6,4},{7,1},{8,10},{9,15},{10,... | collective-permute-start | bytes 393224 | tf_op jit(solution)/shard_map/ppermute | solution.py:27
  43.6 17.0 %collective-permute-start.10 = (bf16[16,32,256]{2,1,0:T(8,128)(2,1)S(1)}, bf16[16,32,256]{2,1,0:T(8,128)(2,1)S(1)}, u32[]{:S(2)}, u32[]{:S(2)}) collective-permute-start(bf16[16,32,256]{2,1,0:T(8,128)(2,1)S(1)} %pad_maximum_fusion.3), channel_id=1, source_target_pairs={{0,6},{1,3},{2,4},{3,1},{4,2},{5,7},{6,0},{7,5},{8,14},{9,11},{10,... | collective-permute-start | bytes 786440 | tf_op jit(solution)/shard_map/ppermute | solution.py:27
  51.6 9.2 %copy-start.1 = (s32[16]{0:T(128)S(1)}, s32[16]{0:T(128)}, u32[]{:S(2)}) copy-start(s32[16]{0:T(128)} %compare_select_fusion.3.meta) | copy-start | bytes 196
  55.4 16.1 %collective-permute-start = (bf16[256,1024]{1,0:T(8,128)(2,1)}, bf16[256,1024]{1,0:T(8,128)(2,1)S(1)}, u32[]{:S(2)}, u32[]{:S(2)}) collective-permute-start(bf16[256,1024]{1,0:T(8,128)(2,1)} %get-tuple-element.12), channel_id=1, source_target_pairs={{0,64},{1,65},{2,66},{3,67},{4,68},{5,69},{6,70},{7,71},{8,72},{9,... | collective-permute-start | bytes 1572872 | tf_op jit(solution)/shard_map/ppermute | solution.py:27
  55.4 16.0 %collective-permute-start.1 = (bf16[256,1024]{1,0:T(8,128)(2,1)}, bf16[256,1024]{1,0:T(8,128)(2,1)S(1)}, u32[]{:S(2)}, u32[]{:S(2)}) collective-permute-start(bf16[256,1024]{1,0:T(8,128)(2,1)} %get-tuple-element.13), channel_id=1, source_target_pairs={{0,128},{1,129},{2,130},{3,131},{4,132},{5,133},{6,134},{7,135},{8... | collective-permute-start | bytes 1572872 | tf_op jit(solution)/shard_map/ppermute | solution.py:27
  60.6 14.0 %collective-permute-start.2 = (bf16[256,1024]{1,0:T(8,128)(2,1)}, bf16[256,1024]{1,0:T(8,128)(2,1)S(1)}, u32[]{:S(2)}, u32[]{:S(2)}) collective-permute-start(bf16[256,1024]{1,0:T(8,128)(2,1)} %get-tuple-element.14), channel_id=1, source_target_pairs={{0,192},{1,193},{2,194},{3,195},{4,196},{5,197},{6,198},{7,199},{8... | collective-permute-start | bytes 1572872 | tf_op jit(solution)/shard_map/ppermute | solution.py:27
  60.7 13.9 %collective-permute-start.11 = (bf16[32,32,256]{2,1,0:T(8,128)(2,1)S(1)}, bf16[32,32,256]{2,1,0:T(8,128)(2,1)S(1)}, u32[]{:S(2)}, u32[]{:S(2)}) collective-permute-start(bf16[32,32,256]{2,1,0:T(8,128)(2,1)S(1)} %pad_maximum_fusion.1.va), channel_id=1, source_target_pairs={{0,1},{1,0},{2,3},{3,2},{4,5},{5,4},{6,7},{7,6},{8,9},{9,8},{10,11... | collective-permute-start | bytes 1572872 | tf_op jit(solution)/shard_map/ppermute | solution.py:27
  74.6 1.0 copy-start
  131.8 1.4 collective-permute-start.12
  133.3 4.4 %collective-permute-start.13 = (bf16[16,8,256]{2,1,0:T(8,128)(2,1)S(1)}, bf16[16,8,256]{2,1,0:T(8,128)(2,1)S(1)}, u32[]{:S(2)}, u32[]{:S(2)}) collective-permute-start(bf16[16,8,256]{2,1,0:T(8,128)(2,1)S(1)} %slice.93), channel_id=1, source_target_pairs={{0,2},{1,7},{2,0},{3,5},{4,6},{5,3},{6,4},{7,1},{8,10},{9,15},{10,... | collective-permute-start | bytes 196616 | tf_op jit(solution)/shard_map/ppermute | solution.py:27
  137.7 5.2 %collective-permute-start.14 = (bf16[16,4,256]{2,1,0:T(4,128)(2,1)S(1)}, bf16[16,4,256]{2,1,0:T(4,128)(2,1)S(1)}, u32[]{:S(2)}, u32[]{:S(2)}) collective-permute-start(bf16[16,4,256]{2,1,0:T(4,128)(2,1)S(1)} %slice.94), channel_id=1, source_target_pairs={{0,6},{1,3},{2,4},{3,1},{4,2},{5,7},{6,0},{7,5},{8,14},{9,11},{10,... | collective-permute-start | bytes 98312 | tf_op jit(solution)/shard_map/ppermute | solution.py:27
  142.9 4.7 %collective-permute-start.15 = (f32[8,4,256]{2,1,0:T(4,128)S(1)}, f32[8,4,256]{2,1,0:T(4,128)S(1)}, u32[]{:S(2)}, u32[]{:S(2)}) collective-permute-start(f32[8,4,256]{2,1,0:T(4,128)S(1)} %slice.75), channel_id=1, source_target_pairs={{0,64},{1,193},{2,66},{3,195},{4,68},{5,197},{6,70},{7,199},{8,72}... | collective-permute-start | bytes 98312 | tf_op jit(solution)/shard_map/ppermute | solution.py:27
  147.7 3.8 %collective-permute-start.16 = (f32[4,4,256]{2,1,0:T(4,128)S(1)}, f32[4,4,256]{2,1,0:T(4,128)S(1)}, u32[]{:S(2)}, u32[]{:S(2)}) collective-permute-start(f32[4,4,256]{2,1,0:T(4,128)S(1)} %slice.77), channel_id=1, source_target_pairs={{0,192},{1,65},{2,194},{3,67},{4,196},{5,69},{6,198},{7,71},{8,200... | collective-permute-start | bytes 49160 | tf_op jit(solution)/shard_map/ppermute | solution.py:27
  151.5 3.7 %collective-permute-start.17 = (f32[4,2,256]{2,1,0:T(2,128)S(1)}, f32[4,2,256]{2,1,0:T(2,128)S(1)}, u32[]{:S(2)}, u32[]{:S(2)}) collective-permute-start(f32[4,2,256]{2,1,0:T(2,128)S(1)} %slice.79), channel_id=1, source_target_pairs={{0,8},{1,9},{2,10},{3,11},{4,12},{5,13},{6,14},{7,15},{8,0},{9,1},... | collective-permute-start | bytes 24584 | tf_op jit(solution)/shard_map/ppermute | solution.py:27
  155.3 4.6 %collective-permute-start.18 = (f32[2,2,256]{2,1,0:T(2,128)S(1)}, f32[2,2,256]{2,1,0:T(2,128)S(1)}, u32[]{:S(2)}, u32[]{:S(2)}) collective-permute-start(f32[2,2,256]{2,1,0:T(2,128)S(1)} %slice.81), channel_id=1, source_target_pairs={{0,16},{1,49},{2,18},{3,51},{4,20},{5,53},{6,22},{7,55},{8,24},{9,... | collective-permute-start | bytes 12296 | tf_op jit(solution)/shard_map/ppermute | solution.py:27
  159.9 5.7 %collective-permute-start.19 = (f32[1,2,256]{2,1,0:T(2,128)S(1)}, f32[1,2,256]{2,1,0:T(2,128)S(1)}, u32[]{:S(2)}, u32[]{:S(2)}) collective-permute-start(f32[1,2,256]{2,1,0:T(2,128)S(1)} %slice.83), channel_id=1, source_target_pairs={{0,48},{1,17},{2,50},{3,19},{4,52},{5,21},{6,54},{7,23},{8,56},{9,... | collective-permute-start | bytes 6152 | tf_op jit(solution)/shard_map/ppermute | solution.py:27

commit v2 on v1

--- a/solution.py
+++ b/solution.py
@@ -56,11 +56,11 @@
     return jnp.concatenate([a, flip(a, dim, mask)], axis=0)
 
 
-def cut_kernel(meta, w, o0, o1, o2, o3, sems):
+def cut_kernel(meta, w, o1, o2, o3, sems):
     x = meta[0]
     copies = []
-    for d, o in enumerate((o0, o1, o2, o3)):
-        at = (x + d) & 3
+    for d, o in enumerate((o1, o2, o3)):
+        at = (x + d + 1) & 3
         for zs in range(2):
             src = w.at[0, :, pl.ds(pl.multiple_of(zs * 2048 + at * 512, 512), 512)]
             dst = o.at[:, zs * 512 : zs * 512 + 512]
@@ -76,15 +76,15 @@
     vm = pl.BlockSpec(memory_space=pltpu.VMEM)
     return pl.pallas_call(
         cut_kernel,
-        out_shape=[jax.ShapeDtypeStruct((256, 1024), BF16)] * 4,
+        out_shape=[jax.ShapeDtypeStruct((256, 1024), BF16)] * 3,
         in_specs=[pl.BlockSpec(memory_space=pltpu.SMEM), hbm],
-        out_specs=[vm] * 4,
-        scratch_shapes=[pltpu.SemaphoreType.DMA((8,))],
+        out_specs=[vm] * 3,
+        scratch_shapes=[pltpu.SemaphoreType.DMA((6,))],
         name="cut",
     )(meta, w)
 
 
-def kernel(meta, w0, w1, w2, w3, va, vb, ct, out, send, vf, blk, back, da, db, ga, gb, wt):
+def kernel(meta, panel, w1, w2, w3, va, vb, out, send, vf, blk, back, da, db, ga, gb, wt, w0, sems):
     x, zh, zl, y, c = meta[0], meta[1], meta[2], meta[3], meta[4]
 
     def place(k, own, far):
@@ -95,8 +95,8 @@
         far_pz = pos_gather(kz ^ zh, 1 - c)
         for zs in range(2):
             rz = zs ^ zl
-            here = (py * 2 + rz) * 4 + pz
-            there = (far_py * 2 + rz) * 4 + far_pz
+            here = pz * 16 + 8 + py * 2 + rz
+            there = far_pz * 16 + 8 + far_py * 2 + rz
             for cs in range(2):
                 src = (own, far)[cs]
                 yield zs, cs, src, jnp.where(c == cs, here, there)
@@ -108,7 +108,7 @@
                 vf[k, :, col : col + 256] = src[idx].astype(F32)
             return 0
 
-        lax.fori_loop(0, 16, body, 0)
+        lax.fori_loop(0, 16, body, 0, unroll=2)
 
     def slot_active(q):
         return (meta[8 + q] % 4) == zh
@@ -128,35 +128,39 @@
 
         def blocks(k, _):
             kx, kz = k // 4, k % 4
-            idx = pos_gather(kz ^ zh, c) * 9 + pos_gather(kx ^ x, c) * 2
-            cond = ct[idx].astype(F32)
-            tri = ct[idx + 1].astype(F32)
+            idx = pos_gather(kz ^ zh, c) * 16 + pos_gather(kx ^ x, c) * 2
+            cond = va[idx].astype(F32)
+            tri = va[idx + 1].astype(F32)
             lhs = jnp.where(same, tri[:, None, :], 0.0).reshape(256, 256).astype(BF16)
             rhs = jnp.broadcast_to(cond[:, None, :], (32, 8, 256)).reshape(256, 256).astype(BF16)
             got = lax.dot_general(lhs, rhs, (((1,), (0,)), ((), ())), preferred_element_type=F32)
             blk[k] = got.astype(BF16).astype(F32)
             return 0
 
-        lax.fori_loop(0, 16, blocks, 0)
+        lax.fori_loop(0, 16, blocks, 0, unroll=4)
 
     def build(dref, k, p, g):
-        own = vf[k]
-        for i in range(16):
-            line = vf[p, pl.ds(g * 16 + i, 1), :]
-            dref[i * 32 : (i + 1) * 32, :] = (own * line).astype(BF16)
+        for j in range(4):
+            ln = slice(j * 256, j * 256 + 256)
+            own = vf[k, :, ln]
+            for i in range(16):
+                line = vf[p, g * 16 + i : g * 16 + i + 1, ln]
+                dref[i * 32 : (i + 1) * 32, ln] = (own * line).astype(BF16)
 
     def multiply(gref, dref):
         gref[...] = lax.dot_general(
             dref[...], wt[...], (((1,), (0,)), ((), ())), preferred_element_type=F32
         )
 
-    def contract(gref, k, p, g):
+    def contract2(k, p):
         for s in range(4):
             acc = [back[k, t * 32 + s * 8 : t * 32 + s * 8 + 8, :] for t in range(8)]
-            for i in range(16):
-                val = gref[i * 32 + s * 8 : i * 32 + s * 8 + 8, :]
+            for i in range(32):
+                gref = ga if i < 16 else gb
+                r = (i % 16) * 32 + s * 8
+                val = gref[r : r + 8, :]
                 for t in range(8):
-                    acc[t] = acc[t] + blk[p, (g * 16 + i) * 8 + t : (g * 16 + i) * 8 + t + 1, :] * val
+                    acc[t] = acc[t] + blk[p, i * 8 + t : i * 8 + t + 1, :] * val
             for t in range(8):
                 back[k, t * 32 + s * 8 : t * 32 + s * 8 + 8, :] = acc[t]
 
@@ -164,6 +168,19 @@
         @pl.when(slot_active(q))
         def _():
             d = (x - meta[8 + q] // 4) & 3
+
+            @pl.when(d == 0)
+            def _():
+                copies = []
+                for zs in range(2):
+                    src = panel.at[0, :, pl.ds(pl.multiple_of(zs * 2048 + x * 512, 512), 512)]
+                    dst = w0.at[:, zs * 512 : zs * 512 + 512]
+                    copies.append(pltpu.make_async_copy(src, dst, sems.at[zs]))
+                for copy in copies:
+                    copy.start()
+                for copy in copies:
+                    copy.wait()
+
             for j, w in enumerate((w0, w1, w2, w3)):
 
                 def turn(w=w):
@@ -180,10 +197,9 @@
                 po = meta[16 + q * 16 + ko]
                 multiply(gb, db)
                 build(da, kc, pc, 0)
-                contract(ga, ko, po, 0)
+                build(db, kc, pc, 1)
+                contract2(ko, po)
                 multiply(ga, da)
-                build(db, kc, pc, 1)
-                contract(gb, ko, po, 1)
                 return 0
 
             lax.fori_loop(0, 17, body, 0)
@@ -202,9 +218,9 @@
 
     def last(k, _):
         kx, kz = k // 4, k % 4
-        idx = pos_gather(kz ^ zh, c) * 9 + pos_gather(kx ^ x, c) * 2
+        idx = pos_gather(kz ^ zh, c) * 16 + pos_gather(kx ^ x, c) * 2
         cond = lax.dot_general(
-            pick, ct[idx], (((1,), (0,)), ((), ())), preferred_element_type=F32
+            pick, va[idx], (((1,), (0,)), ((), ())), preferred_element_type=F32
         ).astype(BF16)
         b = back[k]
         hi = b.astype(BF16)
@@ -218,10 +234,10 @@
         send[far] = res[16:].astype(BF16)
         return 0
 
-    lax.fori_loop(0, 16, last, 0)
-
-
-def local(meta, w0, w1, w2, w3, va, vb, ct):
+    lax.fori_loop(0, 16, last, 0, unroll=4)
+
+
+def local(meta, panel, w1, w2, w3, va, vb):
     vm = pl.BlockSpec(memory_space=pltpu.VMEM)
     return pl.pallas_call(
         kernel,
@@ -229,7 +245,7 @@
             jax.ShapeDtypeStruct((16, 16, 256), F32),
             jax.ShapeDtypeStruct((16, 16, 256), BF16),
         ],
-        in_specs=[pl.BlockSpec(memory_space=pltpu.SMEM)] + [vm] * 7,
+        in_specs=[pl.BlockSpec(memory_space=pltpu.SMEM), pl.BlockSpec(memory_space=pl.ANY)] + [vm] * 5,
         out_specs=[vm, vm],
         scratch_shapes=[
             pltpu.VMEM((16, 32, 1024), F32),
@@ -240,10 +256,12 @@
             pltpu.VMEM((512, 256), F32),
             pltpu.VMEM((512, 256), F32),
             pltpu.VMEM((1024, 256), BF16),
+            pltpu.VMEM((256, 1024), BF16),
+            pltpu.SemaphoreType.DMA((2,)),
         ],
         compiler_params=pltpu.CompilerParams(vmem_limit_bytes=48 << 20),
         name="screened",
-    )(meta, w0, w1, w2, w3, va, vb, ct)
+    )(meta, panel, w1, w2, w3, va, vb)
 
 
 def steps(valence, conduction, trials, w_panels, partner, owner):
@@ -262,27 +280,25 @@
         def shift(v, d=d):
             return [(v[0] + d) % 4] + v[1:]
 
-        got[d] = move(got[d], shift)
-
-    ct = jnp.stack([conduction[0], trials[0]])[None]
-    ct = double(ct, 0, 1)
+        got[d - 1] = move(got[d - 1], shift)
 
     def swap(v):
         return [v[3], v[1], v[2], v[0], v[4]]
 
     va = move(valence, swap)
-
-    ct = double(ct, 0, 3)
-    ct = jnp.concatenate([ct.reshape(8, 32, 256), va], axis=0)
-    ct = double(ct, 1, 1)
-    ct = double(ct, 1, 3)
-    va = ct[8::9]
     va = double(va, 2, 1)
     va = double(va, 3, 1)
     va = double(va, 3, 3)
+
+    ct = jnp.stack([conduction[0], trials[0]])
+    ct = double(ct, 0, 1)
+    ct = double(ct, 0, 3)
+    va = jnp.concatenate([ct, va], axis=0)
+    va = double(va, 1, 1)
+    va = double(va, 1, 3)
     vb = flip(va, 4, 1)
 
-    part, send = local(meta, *got, va, vb, ct)
+    part, send = local(meta, w_panels, *got, va, vb)
 
     part = part + flip(send, 4, 1).astype(F32)
     part = part[:, :8] + flip(part[:, 8:].astype(BF16), 3, 1).astype(F32)

time: 169 us -> 179 us (1.059)
  waiting for transfers between devices: 63.6 us -> 78.6 us
  Pallas kernels: 59.8 us -> 54.8 us
    ppermute x20, waiting for transfers between devices: 63.6 us -> 78.6 us  [move(): return lax.ppermute(a, AXES, pairs)]
    pallas_call x1, Pallas kernels: 56.2 us -> 51.4 us  [local(): pl.pallas_call(kernel, out_shape=[jax.ShapeDtypeStruct((16, 16, 256), F32...]
  transfers between devices with their start and end apart: 20 -> 20, of which waited for: 16 -> 15; matrix products, arithmetic and copies ran while one was open for 0% -> 2% of each run, Pallas kernels for 2% -> 2%
where the time goes in v2:
time: 179 us; the launch traced here: 177 us
  waiting for transfers between devices  78.6 us (44%)
  Pallas kernels  54.8 us (31%)
  starting transfers between devices  39 us (22%)
  local copies, waits for them, and re-layouts  2.48 us (1%)
  other arithmetic  2.18 us (1%)
    ppermute x20, waiting for transfers between devices, move(): return lax.ppermute(a, AXES, pairs)  78.6 us
    pallas_call x1, Pallas kernels, local(): pl.pallas_call(kernel, out_shape=[jax.ShapeDtypeStruct((16, 16, 256), F32...  51.4 us
    ppermute x20, starting transfers between devices, move(): return lax.ppermute(a, AXES, pairs)  39 us
  transfers between devices with their start and end apart: 20, of which 15 were waited for; matrix products, arithmetic and copies ran while one was open for 2% of the time, Pallas kernels for 2%

profile of v2, /device:TPU:2, one launch (start us, length us, event | category | flops | bytes accessed | tf_op | source)
XLA Modules:
  0.0 177.3 jit_solution(11781352054468258066)
XLA Ops:
  0.0 0.7 pad_maximum_fusion.2
  0.7 2.2 %collective-permute-start.3 = (bf16[2,32,256]{2,1,0:T(8,128)(2,1)S(1)}, bf16[2,32,256]{2,1,0:T(8,128)(2,1)S(1)}, u32[]{:S(2)}, u32[]{:S(2)}) collective-permute-start(bf16[2,32,256]{2,1,0:T(8,128)(2,1)S(1)} %pad_maximum_fusion.2), channel_id=1, source_target_pairs={{0,64},{1,193},{2,66},{3,195},{4,68},{5,197},{6,70},{7,199},{8,72}... | collective-permute-start | bytes 98312 | tf_op jit(solution)/shard_map/ppermute | solution.py:27
  3.0 2.7 %collective-permute-start.5 = (bf16[1,32,256]{2,1,0:T(8,128)(2,1)}, bf16[1,32,256]{2,1,0:T(8,128)(2,1)S(1)}, u32[]{:S(2)}, u32[]{:S(2)}) collective-permute-start(bf16[1,32,256]{2,1,0:T(8,128)(2,1)} %param.6), channel_id=1, source_target_pairs={{0,0},{1,1},{2,64},{3,65},{4,128},{5,129},{6,192},{7,193},{8,8},{9... | collective-permute-start | bytes 49160 | tf_op jit(solution)/shard_map/ppermute | solution.py:27
  5.7 0.7 constant_dynamic-update-slice_fusion.16
  6.4 0.7 constant_dynamic-update-slice_fusion.15
  7.1 2.6 %collective-permute-done.5 = bf16[1,32,256]{2,1,0:T(8,128)(2,1)S(1)} collective-permute-done((bf16[1,32,256]{2,1,0:T(8,128)(2,1)}, bf16[1,32,256]{2,1,0:T(8,128)(2,1)S(1)}, u32[]{:S(2)}, u32[]{:S(2)}) %collective-permute-start.5) | collective-permute-done | bytes 16416 | tf_op jit(solution)/shard_map/ppermute | solution.py:27
  9.7 0.2 collective-permute-start.6
  9.9 0.0 collective-permute-done.3
  9.9 0.7 pad_maximum_fusion
  10.7 5.2 %collective-permute-start.4 = (bf16[4,32,256]{2,1,0:T(8,128)(2,1)S(1)}, bf16[4,32,256]{2,1,0:T(8,128)(2,1)S(1)}, u32[]{:S(2)}, u32[]{:S(2)}) collective-permute-start(bf16[4,32,256]{2,1,0:T(8,128)(2,1)S(1)} %pad_maximum_fusion), channel_id=1, source_target_pairs={{0,192},{1,65},{2,194},{3,67},{4,196},{5,69},{6,198},{7,71},{8,200... | collective-permute-start | bytes 196616 | tf_op jit(solution)/shard_map/ppermute | solution.py:27
  15.9 0.0 collective-permute-done.6
  15.9 0.1 collective-permute-start.7
  16.0 3.9 %collective-permute-done.7 = bf16[2,32,256]{2,1,0:T(8,128)(2,1)S(1)} collective-permute-done((bf16[2,32,256]{2,1,0:T(8,128)(2,1)S(1)}, bf16[2,32,256]{2,1,0:T(8,128)(2,1)S(1)}, u32[]{:S(2)}, u32[]{:S(2)}) %collective-permute-start.7) | collective-permute-done | bytes 32800 | tf_op jit(solution)/shard_map/ppermute | solution.py:27
  19.9 1.8 %collective-permute-start.8 = (bf16[4,32,256]{2,1,0:T(8,128)(2,1)S(1)}, bf16[4,32,256]{2,1,0:T(8,128)(2,1)S(1)}, u32[]{:S(2)}, u32[]{:S(2)}) collective-permute-start(bf16[4,32,256]{2,1,0:T(8,128)(2,1)S(1)} %pad_maximum_fusion.1), channel_id=1, source_target_pairs={{0,6},{1,3},{2,4},{3,1},{4,2},{5,7},{6,0},{7,5},{8,14},{9,11},{10,... | collective-permute-start | bytes 196616 | tf_op jit(solution)/shard_map/ppermute | solution.py:27
  21.8 0.0 collective-permute-done.4
  21.9 3.6 %collective-permute-done.8 = bf16[4,32,256]{2,1,0:T(8,128)(2,1)S(1)} collective-permute-done((bf16[4,32,256]{2,1,0:T(8,128)(2,1)S(1)}, bf16[4,32,256]{2,1,0:T(8,128)(2,1)S(1)}, u32[]{:S(2)}, u32[]{:S(2)}) %collective-permute-start.8) | collective-permute-done | bytes 65568 | tf_op jit(solution)/shard_map/ppermute | solution.py:27
  25.5 0.0 copy-start.2
  25.5 0.0 copy-start.3
  25.5 0.0 copy-start
  25.6 3.4 %collective-permute-start.9 = (bf16[16,32,256]{2,1,0:T(8,128)(2,1)S(1)}, bf16[16,32,256]{2,1,0:T(8,128)(2,1)S(1)}, u32[]{:S(2)}, u32[]{:S(2)}) collective-permute-start(bf16[16,32,256]{2,1,0:T(8,128)(2,1)S(1)} %get-tuple-element.19), channel_id=1, source_target_pairs={{0,16},{1,49},{2,18},{3,51},{4,20},{5,53},{6,22},{7,55},{8,24},{9,... | collective-permute-start | bytes 786440 | tf_op jit(solution)/shard_map/ppermute | solution.py:27
  28.9 7.0 %collective-permute-done.9 = bf16[16,32,256]{2,1,0:T(8,128)(2,1)S(1)} collective-permute-done((bf16[16,32,256]{2,1,0:T(8,128)(2,1)S(1)}, bf16[16,32,256]{2,1,0:T(8,128)(2,1)S(1)}, u32[]{:S(2)}, u32[]{:S(2)}) %collective-permute-start.9) | collective-permute-done | bytes 262176 | tf_op jit(solution)/shard_map/ppermute | solution.py:27
  36.0 4.8 %collective-permute-start.10 = (bf16[32,32,256]{2,1,0:T(8,128)(2,1)S(1)}, bf16[32,32,256]{2,1,0:T(8,128)(2,1)S(1)}, u32[]{:S(2)}, u32[]{:S(2)}) collective-permute-start(bf16[32,32,256]{2,1,0:T(8,128)(2,1)S(1)} %get-tuple-element.15), channel_id=1, source_target_pairs={{0,48},{1,17},{2,50},{3,19},{4,52},{5,21},{6,54},{7,23},{8,56},{9,... | collective-permute-start | bytes 1572872 | tf_op jit(solution)/shard_map/ppermute | solution.py:27
  40.8 12.7 %collective-permute-done.10 = bf16[32,32,256]{2,1,0:T(8,128)(2,1)S(1)} collective-permute-done((bf16[32,32,256]{2,1,0:T(8,128)(2,1)S(1)}, bf16[32,32,256]{2,1,0:T(8,128)(2,1)S(1)}, u32[]{:S(2)}, u32[]{:S(2)}) %collective-permute-start.10) | collective-permute-done | bytes 524320 | tf_op jit(solution)/shard_map/ppermute | solution.py:27
  53.6 0.1 collective-permute-start.11
  53.7 0.5 compare_select_fusion.3.meta
  54.2 0.0 copy-start.1
  54.2 3.4 %cut.1 = (bf16[256,1024]{1,0:T(8,128)(2,1)}, bf16[256,1024]{1,0:T(8,128)(2,1)}, bf16[256,1024]{1,0:T(8,128)(2,1)}) custom-call(s32[16]{0:T(128)} %compare_select_fusion.3.meta, bf16[1,256,4096]{2,1,0:T(8,128)(2,1)} %panel.1), custom_call_target="tpu_custom_call" | custom-call | tf_op jit(solution)/shard_map/cut/pallas_call | solution.py:77
  57.6 7.9 %collective-permute-start = (bf16[256,1024]{1,0:T(8,128)(2,1)}, bf16[256,1024]{1,0:T(8,128)(2,1)}, u32[]{:S(2)}, u32[]{:S(2)}) collective-permute-start(bf16[256,1024]{1,0:T(8,128)(2,1)} %get-tuple-element.10), channel_id=1, source_target_pairs={{0,64},{1,65},{2,66},{3,67},{4,68},{5,69},{6,70},{7,71},{8,72},{9,... | collective-permute-start | bytes 1572872 | tf_op jit(solution)/shard_map/ppermute | solution.py:27
  65.5 0.0 collective-permute-start.1
  65.5 2.2 %collective-permute-start.2 = (bf16[256,1024]{1,0:T(8,128)(2,1)}, bf16[256,1024]{1,0:T(8,128)(2,1)}, u32[]{:S(2)}, u32[]{:S(2)}) collective-permute-start(bf16[256,1024]{1,0:T(8,128)(2,1)} %get-tuple-element.12), channel_id=1, source_target_pairs={{0,192},{1,193},{2,194},{3,195},{4,196},{5,197},{6,198},{7,199},{8... | collective-permute-start | bytes 1572872 | tf_op jit(solution)/shard_map/ppermute | solution.py:27
  67.6 0.0 copy-done.1
  67.6 0.1 slice.51
  67.7 0.0 copy-done.2
  67.7 0.1 reshape.9
  67.8 0.0 copy-done.3
  67.8 0.1 pad_add_fusion.meta
  67.9 20.9 %collective-permute-done.w1 = bf16[256,1024]{1,0:T(8,128)(2,1)} collective-permute-done((bf16[256,1024]{1,0:T(8,128)(2,1)}, bf16[256,1024]{1,0:T(8,128)(2,1)}, u32[]{:S(2)}, u32[]{:S(2)}) %collective-permute-start) | collective-permute-done | bytes 524320 | tf_op jit(solution)/shard_map/ppermute | solution.py:27
  88.8 0.0 collective-permute-done.1.w2
  88.8 2.2 %collective-permute-done.2.w3 = bf16[256,1024]{1,0:T(8,128)(2,1)} collective-permute-done((bf16[256,1024]{1,0:T(8,128)(2,1)}, bf16[256,1024]{1,0:T(8,128)(2,1)}, u32[]{:S(2)}, u32[]{:S(2)}) %collective-permute-start.2) | collective-permute-done | bytes 524320 | tf_op jit(solution)/shard_map/ppermute | solution.py:27
  91.0 0.0 collective-permute-done.11.vb
  91.0 0.0 copy-done
  91.0 51.4 %screened.1 = (f32[16,16,256]{2,1,0:T(8,128)S(1)}, bf16[16,16,256]{2,1,0:T(8,128)(2,1)S(1)}) custom-call(s32[64]{0:T(128)S(1)} %pad_add_fusion.meta, bf16[1,256,4096]{2,1,0:T(8,128)(2,1)S(1)} %copy-done, bf16[256,1024]{1,0:T(8,128)(2,1)} %collective-permute-done.w1, bf16[256,1024]{1,0:T(8,128)(2,1)} %collective-permute-done.1.w2, ...), custom_call_target="tpu_custom_call" | custom-call | tf_op jit(solution)/shard_map/screened/pallas_call | solution.py:242
  142.4 0.1 collective-permute-start.12
  142.5 1.3 collective-permute-done.12
  143.9 0.1 collective-permute-start.13
  144.0 4.3 %collective-permute-done.13 = bf16[16,8,256]{2,1,0:T(8,128)(2,1)S(1)} collective-permute-done((bf16[16,8,256]{2,1,0:T(8,128)(2,1)S(1)}, bf16[16,8,256]{2,1,0:T(8,128)(2,1)S(1)}, u32[]{:S(2)}, u32[]{:S(2)}) %collective-permute-start.13) | collective-permute-done | bytes 65568 | tf_op jit(solution)/shard_map/ppermute | solution.py:27
  148.3 2.3 %collective-permute-start.14 = (bf16[16,4,256]{2,1,0:T(4,128)(2,1)S(1)}, bf16[16,4,256]{2,1,0:T(4,128)(2,1)S(1)}, u32[]{:S(2)}, u32[]{:S(2)}) collective-permute-start(bf16[16,4,256]{2,1,0:T(4,128)(2,1)S(1)} %slice.90), channel_id=1, source_target_pairs={{0,6},{1,3},{2,4},{3,1},{4,2},{5,7},{6,0},{7,5},{8,14},{9,11},{10,... | collective-permute-start | bytes 98312 | tf_op jit(solution)/shard_map/ppermute | solution.py:27
  150.6 2.9 %collective-permute-done.14 = bf16[16,4,256]{2,1,0:T(4,128)(2,1)S(1)} collective-permute-done((bf16[16,4,256]{2,1,0:T(4,128)(2,1)S(1)}, bf16[16,4,256]{2,1,0:T(4,128)(2,1)S(1)}, u32[]{:S(2)}, u32[]{:S(2)}) %collective-permute-start.14) | collective-permute-done | bytes 32800 | tf_op jit(solution)/shard_map/ppermute | solution.py:27
  153.5 0.9 collective-permute-start.15
  154.5 3.4 %collective-permute-done.15 = f32[8,4,256]{2,1,0:T(4,128)S(1)} collective-permute-done((f32[8,4,256]{2,1,0:T(4,128)S(1)}, f32[8,4,256]{2,1,0:T(4,128)S(1)}, u32[]{:S(2)}, u32[]{:S(2)}) %collective-permute-start.15) | collective-permute-done | bytes 32800 | tf_op jit(solution)/shard_map/ppermute | solution.py:27
  157.9 2.0 %collective-permute-start.16 = (f32[4,4,256]{2,1,0:T(4,128)S(1)}, f32[4,4,256]{2,1,0:T(4,128)S(1)}, u32[]{:S(2)}, u32[]{:S(2)}) collective-permute-start(f32[4,4,256]{2,1,0:T(4,128)S(1)} %slice.73), channel_id=1, source_target_pairs={{0,192},{1,65},{2,194},{3,67},{4,196},{5,69},{6,198},{7,71},{8,200... | collective-permute-start | bytes 49160 | tf_op jit(solution)/shard_map/ppermute | solution.py:27
  160.0 1.8 %collective-permute-done.16 = f32[4,4,256]{2,1,0:T(4,128)S(1)} collective-permute-done((f32[4,4,256]{2,1,0:T(4,128)S(1)}, f32[4,4,256]{2,1,0:T(4,128)S(1)}, u32[]{:S(2)}, u32[]{:S(2)}) %collective-permute-start.16) | collective-permute-done | bytes 16416 | tf_op jit(solution)/shard_map/ppermute | solution.py:27
  161.8 2.9 %collective-permute-start.17 = (f32[4,2,256]{2,1,0:T(2,128)S(1)}, f32[4,2,256]{2,1,0:T(2,128)S(1)}, u32[]{:S(2)}, u32[]{:S(2)}) collective-permute-start(f32[4,2,256]{2,1,0:T(2,128)S(1)} %slice.75), channel_id=1, source_target_pairs={{0,8},{1,9},{2,10},{3,11},{4,12},{5,13},{6,14},{7,15},{8,0},{9,1},... | collective-permute-start | bytes 24584 | tf_op jit(solution)/shard_map/ppermute | solution.py:27
  164.7 1.6 collective-permute-done.17
  166.3 0.1 collective-permute-start.18
  166.4 4.5 %collective-permute-done.18 = f32[2,2,256]{2,1,0:T(2,128)S(1)} collective-permute-done((f32[2,2,256]{2,1,0:T(2,128)S(1)}, f32[2,2,256]{2,1,0:T(2,128)S(1)}, u32[]{:S(2)}, u32[]{:S(2)}) %collective-permute-start.18) | collective-permute-done | bytes 4128 | tf_op jit(solution)/shard_map/ppermute | solution.py:27
  170.9 0.0 collective-permute-start.19
  171.0 5.7 %collective-permute-done.19 = f32[1,2,256]{2,1,0:T(2,128)S(1)} collective-permute-done((f32[1,2,256]{2,1,0:T(2,128)S(1)}, f32[1,2,256]{2,1,0:T(2,128)S(1)}, u32[]{:S(2)}, u32[]{:S(2)}) %collective-permute-start.19) | collective-permute-done | bytes 2080 | tf_op jit(solution)/shard_map/ppermute | solution.py:27
  176.6 0.7 reshape.10
  (25 shorter events, 0.3 us)
Async XLA Ops:
  0.7 9.2 %collective-permute-start.3 = (bf16[2,32,256]{2,1,0:T(8,128)(2,1)S(1)}, bf16[2,32,256]{2,1,0:T(8,128)(2,1)S(1)}, u32[]{:S(2)}, u32[]{:S(2)}) collective-permute-start(bf16[2,32,256]{2,1,0:T(8,128)(2,1)S(1)} %pad_maximum_fusion.2), channel_id=1, source_target_pairs={{0,64},{1,193},{2,66},{3,195},{4,68},{5,197},{6,70},{7,199},{8,72}... | collective-permute-start | bytes 98312 | tf_op jit(solution)/shard_map/ppermute | solution.py:27
  3.0 6.7 %collective-permute-start.5 = (bf16[1,32,256]{2,1,0:T(8,128)(2,1)}, bf16[1,32,256]{2,1,0:T(8,128)(2,1)S(1)}, u32[]{:S(2)}, u32[]{:S(2)}) collective-permute-start(bf16[1,32,256]{2,1,0:T(8,128)(2,1)} %param.6), channel_id=1, source_target_pairs={{0,0},{1,1},{2,64},{3,65},{4,128},{5,129},{6,192},{7,193},{8,8},{9... | collective-permute-start | bytes 49160 | tf_op jit(solution)/shard_map/ppermute | solution.py:27
  9.7 6.2 %collective-permute-start.6 = (bf16[1,32,256]{2,1,0:T(8,128)(2,1)S(1)}, bf16[1,32,256]{2,1,0:T(8,128)(2,1)S(1)}, u32[]{:S(2)}, u32[]{:S(2)}) collective-permute-start(bf16[1,32,256]{2,1,0:T(8,128)(2,1)S(1)} %collective-permute-done.5), channel_id=1, source_target_pairs={{0,8},{1,9},{2,10},{3,11},{4,12},{5,13},{6,14},{7,15},{8,0},{9,1},... | collective-permute-start | bytes 49160 | tf_op jit(solution)/shard_map/ppermute | solution.py:27
  10.7 11.1 %collective-permute-start.4 = (bf16[4,32,256]{2,1,0:T(8,128)(2,1)S(1)}, bf16[4,32,256]{2,1,0:T(8,128)(2,1)S(1)}, u32[]{:S(2)}, u32[]{:S(2)}) collective-permute-start(bf16[4,32,256]{2,1,0:T(8,128)(2,1)S(1)} %pad_maximum_fusion), channel_id=1, source_target_pairs={{0,192},{1,65},{2,194},{3,67},{4,196},{5,69},{6,198},{7,71},{8,200... | collective-permute-start | bytes 196616 | tf_op jit(solution)/shard_map/ppermute | solution.py:27
  15.9 4.0 %collective-permute-start.7 = (bf16[2,32,256]{2,1,0:T(8,128)(2,1)S(1)}, bf16[2,32,256]{2,1,0:T(8,128)(2,1)S(1)}, u32[]{:S(2)}, u32[]{:S(2)}) collective-permute-start(bf16[2,32,256]{2,1,0:T(8,128)(2,1)S(1)} %pad_maximum_fusion.3), channel_id=1, source_target_pairs={{0,2},{1,7},{2,0},{3,5},{4,6},{5,3},{6,4},{7,1},{8,10},{9,15},{10,... | collective-permute-start | bytes 98312 | tf_op jit(solution)/shard_map/ppermute | solution.py:27
  19.9 5.6 %collective-permute-start.8 = (bf16[4,32,256]{2,1,0:T(8,128)(2,1)S(1)}, bf16[4,32,256]{2,1,0:T(8,128)(2,1)S(1)}, u32[]{:S(2)}, u32[]{:S(2)}) collective-permute-start(bf16[4,32,256]{2,1,0:T(8,128)(2,1)S(1)} %pad_maximum_fusion.1), channel_id=1, source_target_pairs={{0,6},{1,3},{2,4},{3,1},{4,2},{5,7},{6,0},{7,5},{8,14},{9,11},{10,... | collective-permute-start | bytes 196616 | tf_op jit(solution)/shard_map/ppermute | solution.py:27
  25.5 42.2 %copy-start.2 = (s32[3,16]{1,0:T(4,128)S(1)}, s32[3,16]{1,0:T(4,128)}, u32[]{:S(2)}) copy-start(s32[3,16]{1,0:T(4,128)} %param.10) | copy-start | bytes 580
  25.5 42.3 %copy-start.3 = (s32[3]{0:T(128)S(1)}, s32[3]{0:T(128)}, u32[]{:S(2)}) copy-start(s32[3]{0:T(128)} %param.11) | copy-start | bytes 40
  25.5 65.5 %copy-start = (bf16[1,256,4096]{2,1,0:T(8,128)(2,1)S(1)}, bf16[1,256,4096]{2,1,0:T(8,128)(2,1)}, u32[]{:S(2)}) copy-start(bf16[1,256,4096]{2,1,0:T(8,128)(2,1)} %panel.1) | copy-start | bytes 6291460
  25.6 10.4 %collective-permute-start.9 = (bf16[16,32,256]{2,1,0:T(8,128)(2,1)S(1)}, bf16[16,32,256]{2,1,0:T(8,128)(2,1)S(1)}, u32[]{:S(2)}, u32[]{:S(2)}) collective-permute-start(bf16[16,32,256]{2,1,0:T(8,128)(2,1)S(1)} %get-tuple-element.19), channel_id=1, source_target_pairs={{0,16},{1,49},{2,18},{3,51},{4,20},{5,53},{6,22},{7,55},{8,24},{9,... | collective-permute-start | bytes 786440 | tf_op jit(solution)/shard_map/ppermute | solution.py:27
  36.0 17.5 %collective-permute-start.10 = (bf16[32,32,256]{2,1,0:T(8,128)(2,1)S(1)}, bf16[32,32,256]{2,1,0:T(8,128)(2,1)S(1)}, u32[]{:S(2)}, u32[]{:S(2)}) collective-permute-start(bf16[32,32,256]{2,1,0:T(8,128)(2,1)S(1)} %get-tuple-element.15), channel_id=1, source_target_pairs={{0,48},{1,17},{2,50},{3,19},{4,52},{5,21},{6,54},{7,23},{8,56},{9,... | collective-permute-start | bytes 1572872 | tf_op jit(solution)/shard_map/ppermute | solution.py:27
  53.6 37.5 %collective-permute-start.11 = (bf16[64,32,256]{2,1,0:T(8,128)(2,1)S(1)}, bf16[64,32,256]{2,1,0:T(8,128)(2,1)}, u32[]{:S(2)}, u32[]{:S(2)}) collective-permute-start(bf16[64,32,256]{2,1,0:T(8,128)(2,1)S(1)} %constant_dynamic-update-slice_fusion.17.va), channel_id=1, source_target_pairs={{0,1},{1,0},{2,3},{3,2},{4,5},{5,4},{6,7},{7,6},{8,9},{9,8},{10,11... | collective-permute-start | bytes 3145736 | tf_op jit(solution)/shard_map/ppermute | solution.py:27
  54.2 13.4 %copy-start.1 = (s32[16]{0:T(128)S(1)}, s32[16]{0:T(128)}, u32[]{:S(2)}) copy-start(s32[16]{0:T(128)} %compare_select_fusion.3.meta) | copy-start | bytes 196
  57.6 31.2 %collective-permute-start = (bf16[256,1024]{1,0:T(8,128)(2,1)}, bf16[256,1024]{1,0:T(8,128)(2,1)}, u32[]{:S(2)}, u32[]{:S(2)}) collective-permute-start(bf16[256,1024]{1,0:T(8,128)(2,1)} %get-tuple-element.10), channel_id=1, source_target_pairs={{0,64},{1,65},{2,66},{3,67},{4,68},{5,69},{6,70},{7,71},{8,72},{9,... | collective-permute-start | bytes 1572872 | tf_op jit(solution)/shard_map/ppermute | solution.py:27
  65.5 23.3 %collective-permute-start.1 = (bf16[256,1024]{1,0:T(8,128)(2,1)}, bf16[256,1024]{1,0:T(8,128)(2,1)}, u32[]{:S(2)}, u32[]{:S(2)}) collective-permute-start(bf16[256,1024]{1,0:T(8,128)(2,1)} %get-tuple-element.11), channel_id=1, source_target_pairs={{0,128},{1,129},{2,130},{3,131},{4,132},{5,133},{6,134},{7,135},{8... | collective-permute-start | bytes 1572872 | tf_op jit(solution)/shard_map/ppermute | solution.py:27
  65.5 25.5 %collective-permute-start.2 = (bf16[256,1024]{1,0:T(8,128)(2,1)}, bf16[256,1024]{1,0:T(8,128)(2,1)}, u32[]{:S(2)}, u32[]{:S(2)}) collective-permute-start(bf16[256,1024]{1,0:T(8,128)(2,1)} %get-tuple-element.12), channel_id=1, source_target_pairs={{0,192},{1,193},{2,194},{3,195},{4,196},{5,197},{6,198},{7,199},{8... | collective-permute-start | bytes 1572872 | tf_op jit(solution)/shard_map/ppermute | solution.py:27
  142.4 1.4 collective-permute-start.12
  143.9 4.4 %collective-permute-start.13 = (bf16[16,8,256]{2,1,0:T(8,128)(2,1)S(1)}, bf16[16,8,256]{2,1,0:T(8,128)(2,1)S(1)}, u32[]{:S(2)}, u32[]{:S(2)}) collective-permute-start(bf16[16,8,256]{2,1,0:T(8,128)(2,1)S(1)} %slice.89), channel_id=1, source_target_pairs={{0,2},{1,7},{2,0},{3,5},{4,6},{5,3},{6,4},{7,1},{8,10},{9,15},{10,... | collective-permute-start | bytes 196616 | tf_op jit(solution)/shard_map/ppermute | solution.py:27
  148.3 5.2 %collective-permute-start.14 = (bf16[16,4,256]{2,1,0:T(4,128)(2,1)S(1)}, bf16[16,4,256]{2,1,0:T(4,128)(2,1)S(1)}, u32[]{:S(2)}, u32[]{:S(2)}) collective-permute-start(bf16[16,4,256]{2,1,0:T(4,128)(2,1)S(1)} %slice.90), channel_id=1, source_target_pairs={{0,6},{1,3},{2,4},{3,1},{4,2},{5,7},{6,0},{7,5},{8,14},{9,11},{10,... | collective-permute-start | bytes 98312 | tf_op jit(solution)/shard_map/ppermute | solution.py:27
  153.5 4.4 %collective-permute-start.15 = (f32[8,4,256]{2,1,0:T(4,128)S(1)}, f32[8,4,256]{2,1,0:T(4,128)S(1)}, u32[]{:S(2)}, u32[]{:S(2)}) collective-permute-start(f32[8,4,256]{2,1,0:T(4,128)S(1)} %slice.71), channel_id=1, source_target_pairs={{0,64},{1,193},{2,66},{3,195},{4,68},{5,197},{6,70},{7,199},{8,72}... | collective-permute-start | bytes 98312 | tf_op jit(solution)/shard_map/ppermute | solution.py:27
  157.9 3.8 %collective-permute-start.16 = (f32[4,4,256]{2,1,0:T(4,128)S(1)}, f32[4,4,256]{2,1,0:T(4,128)S(1)}, u32[]{:S(2)}, u32[]{:S(2)}) collective-permute-start(f32[4,4,256]{2,1,0:T(4,128)S(1)} %slice.73), channel_id=1, source_target_pairs={{0,192},{1,65},{2,194},{3,67},{4,196},{5,69},{6,198},{7,71},{8,200... | collective-permute-start | bytes 49160 | tf_op jit(solution)/shard_map/ppermute | solution.py:27
  161.8 4.6 %collective-permute-start.17 = (f32[4,2,256]{2,1,0:T(2,128)S(1)}, f32[4,2,256]{2,1,0:T(2,128)S(1)}, u32[]{:S(2)}, u32[]{:S(2)}) collective-permute-start(f32[4,2,256]{2,1,0:T(2,128)S(1)} %slice.75), channel_id=1, source_target_pairs={{0,8},{1,9},{2,10},{3,11},{4,12},{5,13},{6,14},{7,15},{8,0},{9,1},... | collective-permute-start | bytes 24584 | tf_op jit(solution)/shard_map/ppermute | solution.py:27
  166.3 4.6 %collective-permute-start.18 = (f32[2,2,256]{2,1,0:T(2,128)S(1)}, f32[2,2,256]{2,1,0:T(2,128)S(1)}, u32[]{:S(2)}, u32[]{:S(2)}) collective-permute-start(f32[2,2,256]{2,1,0:T(2,128)S(1)} %slice.77), channel_id=1, source_target_pairs={{0,16},{1,49},{2,18},{3,51},{4,20},{5,53},{6,22},{7,55},{8,24},{9,... | collective-permute-start | bytes 12296 | tf_op jit(solution)/shard_map/ppermute | solution.py:27
  170.9 5.7 %collective-permute-start.19 = (f32[1,2,256]{2,1,0:T(2,128)S(1)}, f32[1,2,256]{2,1,0:T(2,128)S(1)}, u32[]{:S(2)}, u32[]{:S(2)}) collective-permute-start(f32[1,2,256]{2,1,0:T(2,128)S(1)} %slice.79), channel_id=1, source_target_pairs={{0,48},{1,17},{2,50},{3,19},{4,52},{5,21},{6,54},{7,23},{8,56},{9,... | collective-permute-start | bytes 6152 | tf_op jit(solution)/shard_map/ppermute | solution.py:27

commit v3 on v2

--- a/solution.py
+++ b/solution.py
@@ -80,6 +80,7 @@
         in_specs=[pl.BlockSpec(memory_space=pltpu.SMEM), hbm],
         out_specs=[vm] * 3,
         scratch_shapes=[pltpu.SemaphoreType.DMA((6,))],
+        compiler_params=pltpu.CompilerParams(vmem_limit_bytes=4 << 20),
         name="cut",
     )(meta, w)
 
@@ -95,8 +96,8 @@
         far_pz = pos_gather(kz ^ zh, 1 - c)
         for zs in range(2):
             rz = zs ^ zl
-            here = pz * 16 + 8 + py * 2 + rz
-            there = far_pz * 16 + 8 + far_py * 2 + rz
+            here = pz * 28 + 12 + (py * 2 + rz) * 2
+            there = far_pz * 28 + 12 + (far_py * 2 + rz) * 2
             for cs in range(2):
                 src = (own, far)[cs]
                 yield zs, cs, src, jnp.where(c == cs, here, there)
@@ -105,7 +106,8 @@
         def body(k, _):
             for zs, cs, src, idx in place(k, first, second):
                 col = (zs * 2 + cs) * 256
-                vf[k, :, col : col + 256] = src[idx].astype(F32)
+                vf[k, :16, col : col + 256] = src[idx].astype(F32)
+                vf[k, 16:, col : col + 256] = src[idx + 1].astype(F32)
             return 0
 
         lax.fori_loop(0, 16, body, 0, unroll=2)
@@ -128,9 +130,13 @@
 
         def blocks(k, _):
             kx, kz = k // 4, k % 4
-            idx = pos_gather(kz ^ zh, c) * 16 + pos_gather(kx ^ x, c) * 2
-            cond = va[idx].astype(F32)
-            tri = va[idx + 1].astype(F32)
+            idx = pos_gather(kz ^ zh, c) * 28 + pos_gather(kx ^ x, c) * 3
+            far = pos_gather(kz ^ zh, 1 - c) * 28 + pos_gather(kx ^ x, 1 - c) * 3
+            cond = jnp.concatenate([va[idx], va[idx + 1]], axis=0).astype(F32)
+            mine, other = va[idx + 2].astype(F32), vb[far + 2].astype(F32)
+            low = jnp.where(c == 0, mine, other)
+            high = jnp.where(c == 0, other, mine)
+            tri = jnp.concatenate([low, high], axis=0)
             lhs = jnp.where(same, tri[:, None, :], 0.0).reshape(256, 256).astype(BF16)
             rhs = jnp.broadcast_to(cond[:, None, :], (32, 8, 256)).reshape(256, 256).astype(BF16)
             got = lax.dot_general(lhs, rhs, (((1,), (0,)), ((), ())), preferred_element_type=F32)
@@ -218,9 +224,10 @@
 
     def last(k, _):
         kx, kz = k // 4, k % 4
-        idx = pos_gather(kz ^ zh, c) * 16 + pos_gather(kx ^ x, c) * 2
+        idx = pos_gather(kz ^ zh, c) * 28 + pos_gather(kx ^ x, c) * 3
+        both = jnp.concatenate([va[idx], va[idx + 1]], axis=0)
         cond = lax.dot_general(
-            pick, va[idx], (((1,), (0,)), ((), ())), preferred_element_type=F32
+            pick, both, (((1,), (0,)), ((), ())), preferred_element_type=F32
         ).astype(BF16)
         b = back[k]
         hi = b.astype(BF16)
@@ -259,7 +266,7 @@
             pltpu.VMEM((256, 1024), BF16),
             pltpu.SemaphoreType.DMA((2,)),
         ],
-        compiler_params=pltpu.CompilerParams(vmem_limit_bytes=48 << 20),
+        compiler_params=pltpu.CompilerParams(vmem_limit_bytes=28 << 20),
         name="screened",
     )(meta, panel, w1, w2, w3, va, vb)
 
@@ -290,10 +297,11 @@
     va = double(va, 3, 1)
     va = double(va, 3, 3)
 
-    ct = jnp.stack([conduction[0], trials[0]])
+    half = lax.dynamic_slice_in_dim(trials[0], c * 16, 16, axis=0)
+    ct = jnp.concatenate([conduction[0], half], axis=0).reshape(3, 16, 256)
     ct = double(ct, 0, 1)
     ct = double(ct, 0, 3)
-    va = jnp.concatenate([ct, va], axis=0)
+    va = jnp.concatenate([ct, va.reshape(16, 16, 256)], axis=0)
     va = double(va, 1, 1)
     va = double(va, 1, 3)
     vb = flip(va, 4, 1)

time: 179 us -> 173 us (0.966)
  waiting for transfers between devices: 78.6 us -> 71.6 us
  starting transfers between devices: 39 us -> 41.8 us
    ppermute x20, waiting for transfers between devices: 78.6 us -> 71.6 us  [move(): return lax.ppermute(a, AXES, pairs)]
    ppermute x20, starting transfers between devices: 39 us -> 41.8 us  [move(): return lax.ppermute(a, AXES, pairs)]
  transfers between devices with their start and end apart: 20 -> 20, of which waited for: 15 -> 16; matrix products, arithmetic and copies ran while one was open for 2% -> 2% of each run, Pallas kernels for 2% -> 1%
where the time goes in v3:
time: 173 us; the launch traced here: 171 us
  waiting for transfers between devices  71.6 us (41%)
  Pallas kernels  53.2 us (31%)
  starting transfers between devices  41.8 us (24%)
  local copies, waits for them, and re-layouts  2.76 us (2%)
    ppermute x20, waiting for transfers between devices, move(): return lax.ppermute(a, AXES, pairs)  71.6 us
    pallas_call x1, Pallas kernels, local(): pl.pallas_call(kernel, out_shape=[jax.ShapeDtypeStruct((16, 16, 256), F32...  51.3 us
    ppermute x20, starting transfers between devices, move(): return lax.ppermute(a, AXES, pairs)  41.8 us
  transfers between devices with their start and end apart: 20, of which 16 were waited for; matrix products, arithmetic and copies ran while one was open for 2% of the time, Pallas kernels for 1%

profile of v3, /device:TPU:2, one launch (start us, length us, event | category | flops | bytes accessed | tf_op | source)
XLA Modules:
  0.0 171.3 jit_solution(16159057210490382301)
XLA Ops:
  0.0 0.0 copy-start
  0.0 0.0 copy-start.1
  0.0 3.6 %collective-permute-start.5 = (bf16[1,32,256]{2,1,0:T(8,128)(2,1)}, bf16[1,32,256]{2,1,0:T(8,128)(2,1)S(1)}, u32[]{:S(2)}, u32[]{:S(2)}) collective-permute-start(bf16[1,32,256]{2,1,0:T(8,128)(2,1)} %param.6), channel_id=1, source_target_pairs={{0,0},{1,1},{2,64},{3,65},{4,128},{5,129},{6,192},{7,193},{8,8},{9... | collective-permute-start | bytes 49160 | tf_op jit(solution)/shard_map/ppermute | solution.py:27
  3.6 0.0 copy-done
  3.6 0.7 pad_maximum_fusion.5
  4.4 0.1 collective-permute-start.3
  4.5 2.4 %collective-permute-done.5 = bf16[1,32,256]{2,1,0:T(8,128)(2,1)S(1)} collective-permute-done((bf16[1,32,256]{2,1,0:T(8,128)(2,1)}, bf16[1,32,256]{2,1,0:T(8,128)(2,1)S(1)}, u32[]{:S(2)}, u32[]{:S(2)}) %collective-permute-start.5) | collective-permute-done | bytes 16416 | tf_op jit(solution)/shard_map/ppermute | solution.py:27
  6.9 1.9 %collective-permute-start.6 = (bf16[1,32,256]{2,1,0:T(8,128)(2,1)S(1)}, bf16[1,32,256]{2,1,0:T(8,128)(2,1)S(1)}, u32[]{:S(2)}, u32[]{:S(2)}) collective-permute-start(bf16[1,32,256]{2,1,0:T(8,128)(2,1)S(1)} %collective-permute-done.5), channel_id=1, source_target_pairs={{0,8},{1,9},{2,10},{3,11},{4,12},{5,13},{6,14},{7,15},{8,0},{9,1},... | collective-permute-start | bytes 49160 | tf_op jit(solution)/shard_map/ppermute | solution.py:27
  8.8 1.8 %collective-permute-done.6 = bf16[1,32,256]{2,1,0:T(8,128)(2,1)S(1)} collective-permute-done((bf16[1,32,256]{2,1,0:T(8,128)(2,1)S(1)}, bf16[1,32,256]{2,1,0:T(8,128)(2,1)S(1)}, u32[]{:S(2)}, u32[]{:S(2)}) %collective-permute-start.6) | collective-permute-done | bytes 16416 | tf_op jit(solution)/shard_map/ppermute | solution.py:27
  10.6 0.0 collective-permute-start.7
  10.6 0.0 collective-permute-done.3
  10.6 4.6 %collective-permute-start.4 = (bf16[6,16,256]{2,1,0:T(8,128)(2,1)S(1)}, bf16[6,16,256]{2,1,0:T(8,128)(2,1)S(1)}, u32[]{:S(2)}, u32[]{:S(2)}) collective-permute-start(bf16[6,16,256]{2,1,0:T(8,128)(2,1)S(1)} %pad_maximum_fusion.3), channel_id=1, source_target_pairs={{0,192},{1,65},{2,194},{3,67},{4,196},{5,69},{6,198},{7,71},{8,200... | collective-permute-start | bytes 147464 | tf_op jit(solution)/shard_map/ppermute | solution.py:27
  15.2 0.0 collective-permute-done.7
  15.2 5.4 %collective-permute-start.8 = (bf16[4,32,256]{2,1,0:T(8,128)(2,1)S(1)}, bf16[4,32,256]{2,1,0:T(8,128)(2,1)S(1)}, u32[]{:S(2)}, u32[]{:S(2)}) collective-permute-start(bf16[4,32,256]{2,1,0:T(8,128)(2,1)S(1)} %pad_maximum_fusion.2), channel_id=1, source_target_pairs={{0,6},{1,3},{2,4},{3,1},{4,2},{5,7},{6,0},{7,5},{8,14},{9,11},{10,... | collective-permute-start | bytes 196616 | tf_op jit(solution)/shard_map/ppermute | solution.py:27
  20.7 2.2 %collective-permute-done.8 = bf16[4,32,256]{2,1,0:T(8,128)(2,1)S(1)} collective-permute-done((bf16[4,32,256]{2,1,0:T(8,128)(2,1)S(1)}, bf16[4,32,256]{2,1,0:T(8,128)(2,1)S(1)}, u32[]{:S(2)}, u32[]{:S(2)}) %collective-permute-start.8) | collective-permute-done | bytes 65568 | tf_op jit(solution)/shard_map/ppermute | solution.py:27
  22.9 0.0 collective-permute-done.4
  23.0 3.4 %collective-permute-start.9 = (bf16[28,16,256]{2,1,0:T(8,128)(2,1)S(1)}, bf16[28,16,256]{2,1,0:T(8,128)(2,1)S(1)}, u32[]{:S(2)}, u32[]{:S(2)}) collective-permute-start(bf16[28,16,256]{2,1,0:T(8,128)(2,1)S(1)} %pad_maximum_fusion), channel_id=1, source_target_pairs={{0,16},{1,49},{2,18},{3,51},{4,20},{5,53},{6,22},{7,55},{8,24},{9,... | collective-permute-start | bytes 688136 | tf_op jit(solution)/shard_map/ppermute | solution.py:27
  26.3 5.3 %collective-permute-done.9 = bf16[28,16,256]{2,1,0:T(8,128)(2,1)S(1)} collective-permute-done((bf16[28,16,256]{2,1,0:T(8,128)(2,1)S(1)}, bf16[28,16,256]{2,1,0:T(8,128)(2,1)S(1)}, u32[]{:S(2)}, u32[]{:S(2)}) %collective-permute-start.9) | collective-permute-done | bytes 229408 | tf_op jit(solution)/shard_map/ppermute | solution.py:27
  31.7 11.7 %collective-permute-start.10 = (bf16[56,16,256]{2,1,0:T(8,128)(2,1)S(1)}, bf16[56,16,256]{2,1,0:T(8,128)(2,1)S(1)}, u32[]{:S(2)}, u32[]{:S(2)}) collective-permute-start(bf16[56,16,256]{2,1,0:T(8,128)(2,1)S(1)} %get-tuple-element.15), channel_id=1, source_target_pairs={{0,48},{1,17},{2,50},{3,19},{4,52},{5,21},{6,54},{7,23},{8,56},{9,... | collective-permute-start | bytes 1376264 | tf_op jit(solution)/shard_map/ppermute | solution.py:27
  43.4 10.9 %collective-permute-done.10 = bf16[56,16,256]{2,1,0:T(8,128)(2,1)S(1)} collective-permute-done((bf16[56,16,256]{2,1,0:T(8,128)(2,1)S(1)}, bf16[56,16,256]{2,1,0:T(8,128)(2,1)S(1)}, u32[]{:S(2)}, u32[]{:S(2)}) %collective-permute-start.10) | collective-permute-done | bytes 458784 | tf_op jit(solution)/shard_map/ppermute | solution.py:27
  54.3 0.1 collective-permute-start.11
  54.5 0.0 copy-done.1
  54.5 0.0 copy-start.2
  54.5 1.9 %cut.1 = (bf16[256,1024]{1,0:T(8,128)(2,1)}, bf16[256,1024]{1,0:T(8,128)(2,1)}, bf16[256,1024]{1,0:T(8,128)(2,1)}) custom-call(s32[16]{0:T(128)S(1)} %compare_select_fusion.3.meta, bf16[1,256,4096]{2,1,0:T(8,128)(2,1)S(1)} %copy-done.1), custom_call_target="tpu_custom_call" | custom-call | tf_op jit(solution)/shard_map/cut/pallas_call | solution.py:77
  56.4 1.8 %collective-permute-start = (bf16[256,1024]{1,0:T(8,128)(2,1)}, bf16[256,1024]{1,0:T(8,128)(2,1)S(1)}, u32[]{:S(2)}, u32[]{:S(2)}) collective-permute-start(bf16[256,1024]{1,0:T(8,128)(2,1)} %get-tuple-element.10), channel_id=1, source_target_pairs={{0,64},{1,65},{2,66},{3,67},{4,68},{5,69},{6,70},{7,71},{8,72},{9,... | collective-permute-start | bytes 1572872 | tf_op jit(solution)/shard_map/ppermute | solution.py:27
  58.2 1.8 %collective-permute-start.1 = (bf16[256,1024]{1,0:T(8,128)(2,1)}, bf16[256,1024]{1,0:T(8,128)(2,1)}, u32[]{:S(2)}, u32[]{:S(2)}) collective-permute-start(bf16[256,1024]{1,0:T(8,128)(2,1)} %get-tuple-element.11), channel_id=1, source_target_pairs={{0,128},{1,129},{2,130},{3,131},{4,132},{5,133},{6,134},{7,135},{8... | collective-permute-start | bytes 1572872 | tf_op jit(solution)/shard_map/ppermute | solution.py:27
  60.0 0.9 collective-permute-start.2
  60.9 0.0 copy-done.2
  60.9 0.6 slice.51
  61.5 1.3 reshape.16
  62.8 0.8 pad_add_fusion.meta
  63.6 7.9 %collective-permute-done.w1 = bf16[256,1024]{1,0:T(8,128)(2,1)S(1)} collective-permute-done((bf16[256,1024]{1,0:T(8,128)(2,1)}, bf16[256,1024]{1,0:T(8,128)(2,1)S(1)}, u32[]{:S(2)}, u32[]{:S(2)}) %collective-permute-start) | collective-permute-done | bytes 524320 | tf_op jit(solution)/shard_map/ppermute | solution.py:27
  71.5 3.4 %collective-permute-done.1.w2 = bf16[256,1024]{1,0:T(8,128)(2,1)} collective-permute-done((bf16[256,1024]{1,0:T(8,128)(2,1)}, bf16[256,1024]{1,0:T(8,128)(2,1)}, u32[]{:S(2)}, u32[]{:S(2)}) %collective-permute-start.1) | collective-permute-done | bytes 524320 | tf_op jit(solution)/shard_map/ppermute | solution.py:27
  74.8 10.4 %collective-permute-done.2.w3 = bf16[256,1024]{1,0:T(8,128)(2,1)} collective-permute-done((bf16[256,1024]{1,0:T(8,128)(2,1)}, bf16[256,1024]{1,0:T(8,128)(2,1)}, u32[]{:S(2)}, u32[]{:S(2)}) %collective-permute-start.2) | collective-permute-done | bytes 524320 | tf_op jit(solution)/shard_map/ppermute | solution.py:27
  85.2 0.0 collective-permute-done.11.vb
  85.2 51.3 %screened.1 = (f32[16,16,256]{2,1,0:T(8,128)S(1)}, bf16[16,16,256]{2,1,0:T(8,128)(2,1)S(1)}) custom-call(s32[64]{0:T(128)S(1)} %pad_add_fusion.meta, bf16[1,256,4096]{2,1,0:T(8,128)(2,1)S(1)} %copy-done.1, bf16[256,1024]{1,0:T(8,128)(2,1)S(1)} %collective-permute-done.w1, bf16[256,1024]{1,0:T(8,128)(2,1)} %collective-permute-done.1.w2, ...), custom_call_target="tpu_custom_call" | custom-call | tf_op jit(solution)/shard_map/screened/pallas_call | solution.py:249
  136.5 0.1 collective-permute-start.12
  136.6 1.3 collective-permute-done.12
  138.0 0.1 collective-permute-start.13
  138.1 4.3 %collective-permute-done.13 = bf16[16,8,256]{2,1,0:T(8,128)(2,1)S(1)} collective-permute-done((bf16[16,8,256]{2,1,0:T(8,128)(2,1)S(1)}, bf16[16,8,256]{2,1,0:T(8,128)(2,1)S(1)}, u32[]{:S(2)}, u32[]{:S(2)}) %collective-permute-start.13) | collective-permute-done | bytes 65568 | tf_op jit(solution)/shard_map/ppermute | solution.py:27
  142.4 1.8 %collective-permute-start.14 = (bf16[16,4,256]{2,1,0:T(4,128)(2,1)S(1)}, bf16[16,4,256]{2,1,0:T(4,128)(2,1)S(1)}, u32[]{:S(2)}, u32[]{:S(2)}) collective-permute-start(bf16[16,4,256]{2,1,0:T(4,128)(2,1)S(1)} %slice.90), channel_id=1, source_target_pairs={{0,6},{1,3},{2,4},{3,1},{4,2},{5,7},{6,0},{7,5},{8,14},{9,11},{10,... | collective-permute-start | bytes 98312 | tf_op jit(solution)/shard_map/ppermute | solution.py:27
  144.2 3.4 %collective-permute-done.14 = bf16[16,4,256]{2,1,0:T(4,128)(2,1)S(1)} collective-permute-done((bf16[16,4,256]{2,1,0:T(4,128)(2,1)S(1)}, bf16[16,4,256]{2,1,0:T(4,128)(2,1)S(1)}, u32[]{:S(2)}, u32[]{:S(2)}) %collective-permute-start.14) | collective-permute-done | bytes 32800 | tf_op jit(solution)/shard_map/ppermute | solution.py:27
  147.7 0.7 collective-permute-start.15
  148.4 3.5 %collective-permute-done.15 = f32[8,4,256]{2,1,0:T(4,128)S(1)} collective-permute-done((f32[8,4,256]{2,1,0:T(4,128)S(1)}, f32[8,4,256]{2,1,0:T(4,128)S(1)}, u32[]{:S(2)}, u32[]{:S(2)}) %collective-permute-start.15) | collective-permute-done | bytes 32800 | tf_op jit(solution)/shard_map/ppermute | solution.py:27
  151.9 0.7 collective-permute-start.16
  152.6 3.1 %collective-permute-done.16 = f32[4,4,256]{2,1,0:T(4,128)S(1)} collective-permute-done((f32[4,4,256]{2,1,0:T(4,128)S(1)}, f32[4,4,256]{2,1,0:T(4,128)S(1)}, u32[]{:S(2)}, u32[]{:S(2)}) %collective-permute-start.16) | collective-permute-done | bytes 16416 | tf_op jit(solution)/shard_map/ppermute | solution.py:27
  155.7 3.0 %collective-permute-start.17 = (f32[4,2,256]{2,1,0:T(2,128)S(1)}, f32[4,2,256]{2,1,0:T(2,128)S(1)}, u32[]{:S(2)}, u32[]{:S(2)}) collective-permute-start(f32[4,2,256]{2,1,0:T(2,128)S(1)} %slice.75), channel_id=1, source_target_pairs={{0,8},{1,9},{2,10},{3,11},{4,12},{5,13},{6,14},{7,15},{8,0},{9,1},... | collective-permute-start | bytes 24584 | tf_op jit(solution)/shard_map/ppermute | solution.py:27
  158.7 1.6 collective-permute-done.17
  160.3 0.1 collective-permute-start.18
  160.4 4.5 %collective-permute-done.18 = f32[2,2,256]{2,1,0:T(2,128)S(1)} collective-permute-done((f32[2,2,256]{2,1,0:T(2,128)S(1)}, f32[2,2,256]{2,1,0:T(2,128)S(1)}, u32[]{:S(2)}, u32[]{:S(2)}) %collective-permute-start.18) | collective-permute-done | bytes 4128 | tf_op jit(solution)/shard_map/ppermute | solution.py:27
  164.9 0.0 collective-permute-start.19
  164.9 5.7 %collective-permute-done.19 = f32[1,2,256]{2,1,0:T(2,128)S(1)} collective-permute-done((f32[1,2,256]{2,1,0:T(2,128)S(1)}, f32[1,2,256]{2,1,0:T(2,128)S(1)}, u32[]{:S(2)}, u32[]{:S(2)}) %collective-permute-start.19) | collective-permute-done | bytes 2080 | tf_op jit(solution)/shard_map/ppermute | solution.py:27
  170.6 0.7 reshape.19
  (28 shorter events, 0.3 us)
Async XLA Ops:
  0.0 3.6 %copy-start = (bf16[1,32,256]{2,1,0:T(8,128)(2,1)S(1)}, bf16[1,32,256]{2,1,0:T(8,128)(2,1)}, u32[]{:S(2)}) copy-start(bf16[1,32,256]{2,1,0:T(8,128)(2,1)} %param.8) | copy-start | bytes 49156
  0.0 54.5 %copy-start.1 = (bf16[1,256,4096]{2,1,0:T(8,128)(2,1)S(1)}, bf16[1,256,4096]{2,1,0:T(8,128)(2,1)}, u32[]{:S(2)}) copy-start(bf16[1,256,4096]{2,1,0:T(8,128)(2,1)} %panel.1) | copy-start | bytes 6291460
  0.0 6.9 %collective-permute-start.5 = (bf16[1,32,256]{2,1,0:T(8,128)(2,1)}, bf16[1,32,256]{2,1,0:T(8,128)(2,1)S(1)}, u32[]{:S(2)}, u32[]{:S(2)}) collective-permute-start(bf16[1,32,256]{2,1,0:T(8,128)(2,1)} %param.6), channel_id=1, source_target_pairs={{0,0},{1,1},{2,64},{3,65},{4,128},{5,129},{6,192},{7,193},{8,8},{9... | collective-permute-start | bytes 49160 | tf_op jit(solution)/shard_map/ppermute | solution.py:27
  4.4 6.3 %collective-permute-start.3 = (bf16[3,16,256]{2,1,0:T(8,128)(2,1)S(1)}, bf16[3,16,256]{2,1,0:T(8,128)(2,1)S(1)}, u32[]{:S(2)}, u32[]{:S(2)}) collective-permute-start(bf16[3,16,256]{2,1,0:T(8,128)(2,1)S(1)} %bitcast.12), channel_id=1, source_target_pairs={{0,64},{1,193},{2,66},{3,195},{4,68},{5,197},{6,70},{7,199},{8,72}... | collective-permute-start | bytes 73736 | tf_op jit(solution)/shard_map/ppermute | solution.py:27
  6.9 3.7 %collective-permute-start.6 = (bf16[1,32,256]{2,1,0:T(8,128)(2,1)S(1)}, bf16[1,32,256]{2,1,0:T(8,128)(2,1)S(1)}, u32[]{:S(2)}, u32[]{:S(2)}) collective-permute-start(bf16[1,32,256]{2,1,0:T(8,128)(2,1)S(1)} %collective-permute-done.5), channel_id=1, source_target_pairs={{0,8},{1,9},{2,10},{3,11},{4,12},{5,13},{6,14},{7,15},{8,0},{9,1},... | collective-permute-start | bytes 49160 | tf_op jit(solution)/shard_map/ppermute | solution.py:27
  10.6 4.6 %collective-permute-start.7 = (bf16[2,32,256]{2,1,0:T(8,128)(2,1)S(1)}, bf16[2,32,256]{2,1,0:T(8,128)(2,1)S(1)}, u32[]{:S(2)}, u32[]{:S(2)}) collective-permute-start(bf16[2,32,256]{2,1,0:T(8,128)(2,1)S(1)} %pad_maximum_fusion.4), channel_id=1, source_target_pairs={{0,2},{1,7},{2,0},{3,5},{4,6},{5,3},{6,4},{7,1},{8,10},{9,15},{10,... | collective-permute-start | bytes 98312 | tf_op jit(solution)/shard_map/ppermute | solution.py:27
  10.6 12.3 %collective-permute-start.4 = (bf16[6,16,256]{2,1,0:T(8,128)(2,1)S(1)}, bf16[6,16,256]{2,1,0:T(8,128)(2,1)S(1)}, u32[]{:S(2)}, u32[]{:S(2)}) collective-permute-start(bf16[6,16,256]{2,1,0:T(8,128)(2,1)S(1)} %pad_maximum_fusion.3), channel_id=1, source_target_pairs={{0,192},{1,65},{2,194},{3,67},{4,196},{5,69},{6,198},{7,71},{8,200... | collective-permute-start | bytes 147464 | tf_op jit(solution)/shard_map/ppermute | solution.py:27
  15.2 7.6 %collective-permute-start.8 = (bf16[4,32,256]{2,1,0:T(8,128)(2,1)S(1)}, bf16[4,32,256]{2,1,0:T(8,128)(2,1)S(1)}, u32[]{:S(2)}, u32[]{:S(2)}) collective-permute-start(bf16[4,32,256]{2,1,0:T(8,128)(2,1)S(1)} %pad_maximum_fusion.2), channel_id=1, source_target_pairs={{0,6},{1,3},{2,4},{3,1},{4,2},{5,7},{6,0},{7,5},{8,14},{9,11},{10,... | collective-permute-start | bytes 196616 | tf_op jit(solution)/shard_map/ppermute | solution.py:27
  23.0 8.7 %collective-permute-start.9 = (bf16[28,16,256]{2,1,0:T(8,128)(2,1)S(1)}, bf16[28,16,256]{2,1,0:T(8,128)(2,1)S(1)}, u32[]{:S(2)}, u32[]{:S(2)}) collective-permute-start(bf16[28,16,256]{2,1,0:T(8,128)(2,1)S(1)} %pad_maximum_fusion), channel_id=1, source_target_pairs={{0,16},{1,49},{2,18},{3,51},{4,20},{5,53},{6,22},{7,55},{8,24},{9,... | collective-permute-start | bytes 688136 | tf_op jit(solution)/shard_map/ppermute | solution.py:27
  31.7 22.6 %collective-permute-start.10 = (bf16[56,16,256]{2,1,0:T(8,128)(2,1)S(1)}, bf16[56,16,256]{2,1,0:T(8,128)(2,1)S(1)}, u32[]{:S(2)}, u32[]{:S(2)}) collective-permute-start(bf16[56,16,256]{2,1,0:T(8,128)(2,1)S(1)} %get-tuple-element.15), channel_id=1, source_target_pairs={{0,48},{1,17},{2,50},{3,19},{4,52},{5,21},{6,54},{7,23},{8,56},{9,... | collective-permute-start | bytes 1376264 | tf_op jit(solution)/shard_map/ppermute | solution.py:27
  54.3 30.9 %collective-permute-start.11 = (bf16[112,16,256]{2,1,0:T(8,128)(2,1)S(1)}, bf16[112,16,256]{2,1,0:T(8,128)(2,1)}, u32[]{:S(2)}, u32[]{:S(2)}) collective-permute-start(bf16[112,16,256]{2,1,0:T(8,128)(2,1)S(1)} %constant_dynamic-update-slice_fusion.5.va), channel_id=1, source_target_pairs={{0,1},{1,0},{2,3},{3,2},{4,5},{5,4},{6,7},{7,6},{8,9},{9,8},{10,11... | collective-permute-start | bytes 2752520 | tf_op jit(solution)/shard_map/ppermute | solution.py:27
  54.5 6.4 %copy-start.2 = (s32[16]{0:T(128)}, s32[16]{0:T(128)S(1)}, u32[]{:S(2)}) copy-start(s32[16]{0:T(128)S(1)} %compare_select_fusion.3.meta) | copy-start | bytes 196
  56.4 15.1 %collective-permute-start = (bf16[256,1024]{1,0:T(8,128)(2,1)}, bf16[256,1024]{1,0:T(8,128)(2,1)S(1)}, u32[]{:S(2)}, u32[]{:S(2)}) collective-permute-start(bf16[256,1024]{1,0:T(8,128)(2,1)} %get-tuple-element.10), channel_id=1, source_target_pairs={{0,64},{1,65},{2,66},{3,67},{4,68},{5,69},{6,70},{7,71},{8,72},{9,... | collective-permute-start | bytes 1572872 | tf_op jit(solution)/shard_map/ppermute | solution.py:27
  58.2 16.7 %collective-permute-start.1 = (bf16[256,1024]{1,0:T(8,128)(2,1)}, bf16[256,1024]{1,0:T(8,128)(2,1)}, u32[]{:S(2)}, u32[]{:S(2)}) collective-permute-start(bf16[256,1024]{1,0:T(8,128)(2,1)} %get-tuple-element.11), channel_id=1, source_target_pairs={{0,128},{1,129},{2,130},{3,131},{4,132},{5,133},{6,134},{7,135},{8... | collective-permute-start | bytes 1572872 | tf_op jit(solution)/shard_map/ppermute | solution.py:27
  60.0 25.2 %collective-permute-start.2 = (bf16[256,1024]{1,0:T(8,128)(2,1)}, bf16[256,1024]{1,0:T(8,128)(2,1)}, u32[]{:S(2)}, u32[]{:S(2)}) collective-permute-start(bf16[256,1024]{1,0:T(8,128)(2,1)} %get-tuple-element.12), channel_id=1, source_target_pairs={{0,192},{1,193},{2,194},{3,195},{4,196},{5,197},{6,198},{7,199},{8... | collective-permute-start | bytes 1572872 | tf_op jit(solution)/shard_map/ppermute | solution.py:27
  136.5 1.4 collective-permute-start.12
  138.0 4.4 %collective-permute-start.13 = (bf16[16,8,256]{2,1,0:T(8,128)(2,1)S(1)}, bf16[16,8,256]{2,1,0:T(8,128)(2,1)S(1)}, u32[]{:S(2)}, u32[]{:S(2)}) collective-permute-start(bf16[16,8,256]{2,1,0:T(8,128)(2,1)S(1)} %slice.89), channel_id=1, source_target_pairs={{0,2},{1,7},{2,0},{3,5},{4,6},{5,3},{6,4},{7,1},{8,10},{9,15},{10,... | collective-permute-start | bytes 196616 | tf_op jit(solution)/shard_map/ppermute | solution.py:27
  142.4 5.2 %collective-permute-start.14 = (bf16[16,4,256]{2,1,0:T(4,128)(2,1)S(1)}, bf16[16,4,256]{2,1,0:T(4,128)(2,1)S(1)}, u32[]{:S(2)}, u32[]{:S(2)}) collective-permute-start(bf16[16,4,256]{2,1,0:T(4,128)(2,1)S(1)} %slice.90), channel_id=1, source_target_pairs={{0,6},{1,3},{2,4},{3,1},{4,2},{5,7},{6,0},{7,5},{8,14},{9,11},{10,... | collective-permute-start | bytes 98312 | tf_op jit(solution)/shard_map/ppermute | solution.py:27
  147.7 4.2 %collective-permute-start.15 = (f32[8,4,256]{2,1,0:T(4,128)S(1)}, f32[8,4,256]{2,1,0:T(4,128)S(1)}, u32[]{:S(2)}, u32[]{:S(2)}) collective-permute-start(f32[8,4,256]{2,1,0:T(4,128)S(1)} %slice.71), channel_id=1, source_target_pairs={{0,64},{1,193},{2,66},{3,195},{4,68},{5,197},{6,70},{7,199},{8,72}... | collective-permute-start | bytes 98312 | tf_op jit(solution)/shard_map/ppermute | solution.py:27
  151.9 3.8 %collective-permute-start.16 = (f32[4,4,256]{2,1,0:T(4,128)S(1)}, f32[4,4,256]{2,1,0:T(4,128)S(1)}, u32[]{:S(2)}, u32[]{:S(2)}) collective-permute-start(f32[4,4,256]{2,1,0:T(4,128)S(1)} %slice.73), channel_id=1, source_target_pairs={{0,192},{1,65},{2,194},{3,67},{4,196},{5,69},{6,198},{7,71},{8,200... | collective-permute-start | bytes 49160 | tf_op jit(solution)/shard_map/ppermute | solution.py:27
  155.7 4.6 %collective-permute-start.17 = (f32[4,2,256]{2,1,0:T(2,128)S(1)}, f32[4,2,256]{2,1,0:T(2,128)S(1)}, u32[]{:S(2)}, u32[]{:S(2)}) collective-permute-start(f32[4,2,256]{2,1,0:T(2,128)S(1)} %slice.75), channel_id=1, source_target_pairs={{0,8},{1,9},{2,10},{3,11},{4,12},{5,13},{6,14},{7,15},{8,0},{9,1},... | collective-permute-start | bytes 24584 | tf_op jit(solution)/shard_map/ppermute | solution.py:27
  160.3 4.6 %collective-permute-start.18 = (f32[2,2,256]{2,1,0:T(2,128)S(1)}, f32[2,2,256]{2,1,0:T(2,128)S(1)}, u32[]{:S(2)}, u32[]{:S(2)}) collective-permute-start(f32[2,2,256]{2,1,0:T(2,128)S(1)} %slice.77), channel_id=1, source_target_pairs={{0,16},{1,49},{2,18},{3,51},{4,20},{5,53},{6,22},{7,55},{8,24},{9,... | collective-permute-start | bytes 12296 | tf_op jit(solution)/shard_map/ppermute | solution.py:27
  164.9 5.7 %collective-permute-start.19 = (f32[1,2,256]{2,1,0:T(2,128)S(1)}, f32[1,2,256]{2,1,0:T(2,128)S(1)}, u32[]{:S(2)}, u32[]{:S(2)}) collective-permute-start(f32[1,2,256]{2,1,0:T(2,128)S(1)} %slice.79), channel_id=1, source_target_pairs={{0,48},{1,17},{2,50},{3,19},{4,52},{5,21},{6,54},{7,23},{8,56},{9,... | collective-permute-start | bytes 6152 | tf_op jit(solution)/shard_map/ppermute | solution.py:27

commit v4 on v2

--- a/solution.py
+++ b/solution.py
@@ -187,22 +187,25 @@
                     wt[...] = w[...].T
 
                 pl.when(d == j)(turn)
-            db[...] = jnp.zeros_like(db)
-            ga[...] = jnp.zeros_like(ga)
+
+            def mate(k):
+                return meta[16 + q * 16 + k]
+
+            build(da, 0, mate(0), 0)
+            build(db, 0, mate(0), 1)
+            multiply(ga, da)
 
             def body(k, _):
-                kc = jnp.minimum(k, 15)
-                pc = meta[16 + q * 16 + kc]
-                ko = jnp.maximum(k - 1, 0)
-                po = meta[16 + q * 16 + ko]
                 multiply(gb, db)
-                build(da, kc, pc, 0)
-                build(db, kc, pc, 1)
-                contract2(ko, po)
+                build(da, k, mate(k), 0)
+                build(db, k, mate(k), 1)
+                contract2(k - 1, mate(k - 1))
                 multiply(ga, da)
                 return 0
 
-            lax.fori_loop(0, 17, body, 0)
+            lax.fori_loop(1, 16, body, 0)
+            multiply(gb, db)
+            contract2(15, mate(15))
 
         return 0
 

time: 179 us -> 177 us (0.989)
  Pallas kernels: 54.8 us -> 52.1 us
    pallas_call x1, Pallas kernels: 51.4 us -> 48.8 us  [local(): pl.pallas_call(kernel, out_shape=[jax.ShapeDtypeStruct((16, 16, 256), F32...]
where the time goes in v4:
time: 177 us; the launch traced here: 175 us
  waiting for transfers between devices  78.5 us (44%)
  Pallas kernels  52.1 us (29%)
  starting transfers between devices  39.1 us (22%)
  local copies, waits for them, and re-layouts  2.48 us (1%)
  other arithmetic  2.18 us (1%)
    ppermute x20, waiting for transfers between devices, move(): return lax.ppermute(a, AXES, pairs)  78.5 us
    pallas_call x1, Pallas kernels, local(): pl.pallas_call(kernel, out_shape=[jax.ShapeDtypeStruct((16, 16, 256), F32...  48.8 us
    ppermute x20, starting transfers between devices, move(): return lax.ppermute(a, AXES, pairs)  39.1 us
  transfers between devices with their start and end apart: 20, of which 15 were waited for; matrix products, arithmetic and copies ran while one was open for 2% of the time, Pallas kernels for 2%

profile of v4, /device:TPU:2, one launch (start us, length us, event | category | flops | bytes accessed | tf_op | source)
XLA Modules:
  0.0 174.7 jit_solution(7657092592329690392)
XLA Ops:
  0.0 0.7 pad_maximum_fusion.2
  0.7 2.2 %collective-permute-start.3 = (bf16[2,32,256]{2,1,0:T(8,128)(2,1)S(1)}, bf16[2,32,256]{2,1,0:T(8,128)(2,1)S(1)}, u32[]{:S(2)}, u32[]{:S(2)}) collective-permute-start(bf16[2,32,256]{2,1,0:T(8,128)(2,1)S(1)} %pad_maximum_fusion.2), channel_id=1, source_target_pairs={{0,64},{1,193},{2,66},{3,195},{4,68},{5,197},{6,70},{7,199},{8,72}... | collective-permute-start | bytes 98312 | tf_op jit(solution)/shard_map/ppermute | solution.py:27
  3.0 2.7 %collective-permute-start.5 = (bf16[1,32,256]{2,1,0:T(8,128)(2,1)}, bf16[1,32,256]{2,1,0:T(8,128)(2,1)S(1)}, u32[]{:S(2)}, u32[]{:S(2)}) collective-permute-start(bf16[1,32,256]{2,1,0:T(8,128)(2,1)} %param.6), channel_id=1, source_target_pairs={{0,0},{1,1},{2,64},{3,65},{4,128},{5,129},{6,192},{7,193},{8,8},{9... | collective-permute-start | bytes 49160 | tf_op jit(solution)/shard_map/ppermute | solution.py:27
  5.7 0.7 constant_dynamic-update-slice_fusion.16
  6.4 0.7 constant_dynamic-update-slice_fusion.15
  7.1 2.6 %collective-permute-done.5 = bf16[1,32,256]{2,1,0:T(8,128)(2,1)S(1)} collective-permute-done((bf16[1,32,256]{2,1,0:T(8,128)(2,1)}, bf16[1,32,256]{2,1,0:T(8,128)(2,1)S(1)}, u32[]{:S(2)}, u32[]{:S(2)}) %collective-permute-start.5) | collective-permute-done | bytes 16416 | tf_op jit(solution)/shard_map/ppermute | solution.py:27
  9.7 0.2 collective-permute-start.6
  9.9 0.0 collective-permute-done.3
  9.9 0.7 pad_maximum_fusion
  10.7 5.2 %collective-permute-start.4 = (bf16[4,32,256]{2,1,0:T(8,128)(2,1)S(1)}, bf16[4,32,256]{2,1,0:T(8,128)(2,1)S(1)}, u32[]{:S(2)}, u32[]{:S(2)}) collective-permute-start(bf16[4,32,256]{2,1,0:T(8,128)(2,1)S(1)} %pad_maximum_fusion), channel_id=1, source_target_pairs={{0,192},{1,65},{2,194},{3,67},{4,196},{5,69},{6,198},{7,71},{8,200... | collective-permute-start | bytes 196616 | tf_op jit(solution)/shard_map/ppermute | solution.py:27
  15.9 0.0 collective-permute-done.6
  15.9 0.1 collective-permute-start.7
  16.0 3.9 %collective-permute-done.7 = bf16[2,32,256]{2,1,0:T(8,128)(2,1)S(1)} collective-permute-done((bf16[2,32,256]{2,1,0:T(8,128)(2,1)S(1)}, bf16[2,32,256]{2,1,0:T(8,128)(2,1)S(1)}, u32[]{:S(2)}, u32[]{:S(2)}) %collective-permute-start.7) | collective-permute-done | bytes 32800 | tf_op jit(solution)/shard_map/ppermute | solution.py:27
  19.9 1.8 %collective-permute-start.8 = (bf16[4,32,256]{2,1,0:T(8,128)(2,1)S(1)}, bf16[4,32,256]{2,1,0:T(8,128)(2,1)S(1)}, u32[]{:S(2)}, u32[]{:S(2)}) collective-permute-start(bf16[4,32,256]{2,1,0:T(8,128)(2,1)S(1)} %pad_maximum_fusion.1), channel_id=1, source_target_pairs={{0,6},{1,3},{2,4},{3,1},{4,2},{5,7},{6,0},{7,5},{8,14},{9,11},{10,... | collective-permute-start | bytes 196616 | tf_op jit(solution)/shard_map/ppermute | solution.py:27
  21.8 0.0 collective-permute-done.4
  21.9 3.6 %collective-permute-done.8 = bf16[4,32,256]{2,1,0:T(8,128)(2,1)S(1)} collective-permute-done((bf16[4,32,256]{2,1,0:T(8,128)(2,1)S(1)}, bf16[4,32,256]{2,1,0:T(8,128)(2,1)S(1)}, u32[]{:S(2)}, u32[]{:S(2)}) %collective-permute-start.8) | collective-permute-done | bytes 65568 | tf_op jit(solution)/shard_map/ppermute | solution.py:27
  25.5 0.0 copy-start.2
  25.5 0.0 copy-start.3
  25.5 0.0 copy-start
  25.6 3.4 %collective-permute-start.9 = (bf16[16,32,256]{2,1,0:T(8,128)(2,1)S(1)}, bf16[16,32,256]{2,1,0:T(8,128)(2,1)S(1)}, u32[]{:S(2)}, u32[]{:S(2)}) collective-permute-start(bf16[16,32,256]{2,1,0:T(8,128)(2,1)S(1)} %get-tuple-element.19), channel_id=1, source_target_pairs={{0,16},{1,49},{2,18},{3,51},{4,20},{5,53},{6,22},{7,55},{8,24},{9,... | collective-permute-start | bytes 786440 | tf_op jit(solution)/shard_map/ppermute | solution.py:27
  28.9 7.0 %collective-permute-done.9 = bf16[16,32,256]{2,1,0:T(8,128)(2,1)S(1)} collective-permute-done((bf16[16,32,256]{2,1,0:T(8,128)(2,1)S(1)}, bf16[16,32,256]{2,1,0:T(8,128)(2,1)S(1)}, u32[]{:S(2)}, u32[]{:S(2)}) %collective-permute-start.9) | collective-permute-done | bytes 262176 | tf_op jit(solution)/shard_map/ppermute | solution.py:27
  36.0 4.8 %collective-permute-start.10 = (bf16[32,32,256]{2,1,0:T(8,128)(2,1)S(1)}, bf16[32,32,256]{2,1,0:T(8,128)(2,1)S(1)}, u32[]{:S(2)}, u32[]{:S(2)}) collective-permute-start(bf16[32,32,256]{2,1,0:T(8,128)(2,1)S(1)} %get-tuple-element.15), channel_id=1, source_target_pairs={{0,48},{1,17},{2,50},{3,19},{4,52},{5,21},{6,54},{7,23},{8,56},{9,... | collective-permute-start | bytes 1572872 | tf_op jit(solution)/shard_map/ppermute | solution.py:27
  40.8 12.7 %collective-permute-done.10 = bf16[32,32,256]{2,1,0:T(8,128)(2,1)S(1)} collective-permute-done((bf16[32,32,256]{2,1,0:T(8,128)(2,1)S(1)}, bf16[32,32,256]{2,1,0:T(8,128)(2,1)S(1)}, u32[]{:S(2)}, u32[]{:S(2)}) %collective-permute-start.10) | collective-permute-done | bytes 524320 | tf_op jit(solution)/shard_map/ppermute | solution.py:27
  53.6 0.1 collective-permute-start.11
  53.7 0.5 compare_select_fusion.3.meta
  54.2 0.0 copy-start.1
  54.2 3.4 %cut.1 = (bf16[256,1024]{1,0:T(8,128)(2,1)}, bf16[256,1024]{1,0:T(8,128)(2,1)}, bf16[256,1024]{1,0:T(8,128)(2,1)}) custom-call(s32[16]{0:T(128)} %compare_select_fusion.3.meta, bf16[1,256,4096]{2,1,0:T(8,128)(2,1)} %panel.1), custom_call_target="tpu_custom_call" | custom-call | tf_op jit(solution)/shard_map/cut/pallas_call | solution.py:77
  57.6 7.9 %collective-permute-start = (bf16[256,1024]{1,0:T(8,128)(2,1)}, bf16[256,1024]{1,0:T(8,128)(2,1)}, u32[]{:S(2)}, u32[]{:S(2)}) collective-permute-start(bf16[256,1024]{1,0:T(8,128)(2,1)} %get-tuple-element.10), channel_id=1, source_target_pairs={{0,64},{1,65},{2,66},{3,67},{4,68},{5,69},{6,70},{7,71},{8,72},{9,... | collective-permute-start | bytes 1572872 | tf_op jit(solution)/shard_map/ppermute | solution.py:27
  65.5 0.0 collective-permute-start.1
  65.5 2.2 %collective-permute-start.2 = (bf16[256,1024]{1,0:T(8,128)(2,1)}, bf16[256,1024]{1,0:T(8,128)(2,1)}, u32[]{:S(2)}, u32[]{:S(2)}) collective-permute-start(bf16[256,1024]{1,0:T(8,128)(2,1)} %get-tuple-element.12), channel_id=1, source_target_pairs={{0,192},{1,193},{2,194},{3,195},{4,196},{5,197},{6,198},{7,199},{8... | collective-permute-start | bytes 1572872 | tf_op jit(solution)/shard_map/ppermute | solution.py:27
  67.6 0.0 copy-done.1
  67.6 0.1 slice.51
  67.7 0.0 copy-done.2
  67.7 0.1 reshape.9
  67.8 0.0 copy-done.3
  67.8 0.1 pad_add_fusion.meta
  67.9 20.9 %collective-permute-done.w1 = bf16[256,1024]{1,0:T(8,128)(2,1)} collective-permute-done((bf16[256,1024]{1,0:T(8,128)(2,1)}, bf16[256,1024]{1,0:T(8,128)(2,1)}, u32[]{:S(2)}, u32[]{:S(2)}) %collective-permute-start) | collective-permute-done | bytes 524320 | tf_op jit(solution)/shard_map/ppermute | solution.py:27
  88.8 0.0 collective-permute-done.1.w2
  88.8 2.2 %collective-permute-done.2.w3 = bf16[256,1024]{1,0:T(8,128)(2,1)} collective-permute-done((bf16[256,1024]{1,0:T(8,128)(2,1)}, bf16[256,1024]{1,0:T(8,128)(2,1)}, u32[]{:S(2)}, u32[]{:S(2)}) %collective-permute-start.2) | collective-permute-done | bytes 524320 | tf_op jit(solution)/shard_map/ppermute | solution.py:27
  91.0 0.0 collective-permute-done.11.vb
  91.0 0.0 copy-done
  91.0 48.8 %screened.1 = (f32[16,16,256]{2,1,0:T(8,128)S(1)}, bf16[16,16,256]{2,1,0:T(8,128)(2,1)S(1)}) custom-call(s32[64]{0:T(128)S(1)} %pad_add_fusion.meta, bf16[1,256,4096]{2,1,0:T(8,128)(2,1)S(1)} %copy-done, bf16[256,1024]{1,0:T(8,128)(2,1)} %collective-permute-done.w1, bf16[256,1024]{1,0:T(8,128)(2,1)} %collective-permute-done.1.w2, ...), custom_call_target="tpu_custom_call" | custom-call | tf_op jit(solution)/shard_map/screened/pallas_call | solution.py:245
  139.8 0.1 collective-permute-start.12
  139.9 1.3 collective-permute-done.12
  141.3 0.3 collective-permute-start.13
  141.6 4.3 %collective-permute-done.13 = bf16[16,8,256]{2,1,0:T(8,128)(2,1)S(1)} collective-permute-done((bf16[16,8,256]{2,1,0:T(8,128)(2,1)S(1)}, bf16[16,8,256]{2,1,0:T(8,128)(2,1)S(1)}, u32[]{:S(2)}, u32[]{:S(2)}) %collective-permute-start.13) | collective-permute-done | bytes 65568 | tf_op jit(solution)/shard_map/ppermute | solution.py:27
  145.9 2.3 %collective-permute-start.14 = (bf16[16,4,256]{2,1,0:T(4,128)(2,1)S(1)}, bf16[16,4,256]{2,1,0:T(4,128)(2,1)S(1)}, u32[]{:S(2)}, u32[]{:S(2)}) collective-permute-start(bf16[16,4,256]{2,1,0:T(4,128)(2,1)S(1)} %slice.90), channel_id=1, source_target_pairs={{0,6},{1,3},{2,4},{3,1},{4,2},{5,7},{6,0},{7,5},{8,14},{9,11},{10,... | collective-permute-start | bytes 98312 | tf_op jit(solution)/shard_map/ppermute | solution.py:27
  148.1 2.9 %collective-permute-done.14 = bf16[16,4,256]{2,1,0:T(4,128)(2,1)S(1)} collective-permute-done((bf16[16,4,256]{2,1,0:T(4,128)(2,1)S(1)}, bf16[16,4,256]{2,1,0:T(4,128)(2,1)S(1)}, u32[]{:S(2)}, u32[]{:S(2)}) %collective-permute-start.14) | collective-permute-done | bytes 32800 | tf_op jit(solution)/shard_map/ppermute | solution.py:27
  151.1 0.8 collective-permute-start.15
  151.9 3.4 %collective-permute-done.15 = f32[8,4,256]{2,1,0:T(4,128)S(1)} collective-permute-done((f32[8,4,256]{2,1,0:T(4,128)S(1)}, f32[8,4,256]{2,1,0:T(4,128)S(1)}, u32[]{:S(2)}, u32[]{:S(2)}) %collective-permute-start.15) | collective-permute-done | bytes 32800 | tf_op jit(solution)/shard_map/ppermute | solution.py:27
  155.3 2.1 %collective-permute-start.16 = (f32[4,4,256]{2,1,0:T(4,128)S(1)}, f32[4,4,256]{2,1,0:T(4,128)S(1)}, u32[]{:S(2)}, u32[]{:S(2)}) collective-permute-start(f32[4,4,256]{2,1,0:T(4,128)S(1)} %slice.73), channel_id=1, source_target_pairs={{0,192},{1,65},{2,194},{3,67},{4,196},{5,69},{6,198},{7,71},{8,200... | collective-permute-start | bytes 49160 | tf_op jit(solution)/shard_map/ppermute | solution.py:27
  157.4 1.7 collective-permute-done.16
  159.1 2.9 %collective-permute-start.17 = (f32[4,2,256]{2,1,0:T(2,128)S(1)}, f32[4,2,256]{2,1,0:T(2,128)S(1)}, u32[]{:S(2)}, u32[]{:S(2)}) collective-permute-start(f32[4,2,256]{2,1,0:T(2,128)S(1)} %slice.75), channel_id=1, source_target_pairs={{0,8},{1,9},{2,10},{3,11},{4,12},{5,13},{6,14},{7,15},{8,0},{9,1},... | collective-permute-start | bytes 24584 | tf_op jit(solution)/shard_map/ppermute | solution.py:27
  162.1 1.6 collective-permute-done.17
  163.7 0.1 collective-permute-start.18
  163.8 4.5 %collective-permute-done.18 = f32[2,2,256]{2,1,0:T(2,128)S(1)} collective-permute-done((f32[2,2,256]{2,1,0:T(2,128)S(1)}, f32[2,2,256]{2,1,0:T(2,128)S(1)}, u32[]{:S(2)}, u32[]{:S(2)}) %collective-permute-start.18) | collective-permute-done | bytes 4128 | tf_op jit(solution)/shard_map/ppermute | solution.py:27
  168.3 0.0 collective-permute-start.19
  168.3 5.7 %collective-permute-done.19 = f32[1,2,256]{2,1,0:T(2,128)S(1)} collective-permute-done((f32[1,2,256]{2,1,0:T(2,128)S(1)}, f32[1,2,256]{2,1,0:T(2,128)S(1)}, u32[]{:S(2)}, u32[]{:S(2)}) %collective-permute-start.19) | collective-permute-done | bytes 2080 | tf_op jit(solution)/shard_map/ppermute | solution.py:27
  174.0 0.7 reshape.10
  (25 shorter events, 0.3 us)
Async XLA Ops:
  0.7 9.2 %collective-permute-start.3 = (bf16[2,32,256]{2,1,0:T(8,128)(2,1)S(1)}, bf16[2,32,256]{2,1,0:T(8,128)(2,1)S(1)}, u32[]{:S(2)}, u32[]{:S(2)}) collective-permute-start(bf16[2,32,256]{2,1,0:T(8,128)(2,1)S(1)} %pad_maximum_fusion.2), channel_id=1, source_target_pairs={{0,64},{1,193},{2,66},{3,195},{4,68},{5,197},{6,70},{7,199},{8,72}... | collective-permute-start | bytes 98312 | tf_op jit(solution)/shard_map/ppermute | solution.py:27
  3.0 6.7 %collective-permute-start.5 = (bf16[1,32,256]{2,1,0:T(8,128)(2,1)}, bf16[1,32,256]{2,1,0:T(8,128)(2,1)S(1)}, u32[]{:S(2)}, u32[]{:S(2)}) collective-permute-start(bf16[1,32,256]{2,1,0:T(8,128)(2,1)} %param.6), channel_id=1, source_target_pairs={{0,0},{1,1},{2,64},{3,65},{4,128},{5,129},{6,192},{7,193},{8,8},{9... | collective-permute-start | bytes 49160 | tf_op jit(solution)/shard_map/ppermute | solution.py:27
  9.7 6.2 %collective-permute-start.6 = (bf16[1,32,256]{2,1,0:T(8,128)(2,1)S(1)}, bf16[1,32,256]{2,1,0:T(8,128)(2,1)S(1)}, u32[]{:S(2)}, u32[]{:S(2)}) collective-permute-start(bf16[1,32,256]{2,1,0:T(8,128)(2,1)S(1)} %collective-permute-done.5), channel_id=1, source_target_pairs={{0,8},{1,9},{2,10},{3,11},{4,12},{5,13},{6,14},{7,15},{8,0},{9,1},... | collective-permute-start | bytes 49160 | tf_op jit(solution)/shard_map/ppermute | solution.py:27
  10.7 11.1 %collective-permute-start.4 = (bf16[4,32,256]{2,1,0:T(8,128)(2,1)S(1)}, bf16[4,32,256]{2,1,0:T(8,128)(2,1)S(1)}, u32[]{:S(2)}, u32[]{:S(2)}) collective-permute-start(bf16[4,32,256]{2,1,0:T(8,128)(2,1)S(1)} %pad_maximum_fusion), channel_id=1, source_target_pairs={{0,192},{1,65},{2,194},{3,67},{4,196},{5,69},{6,198},{7,71},{8,200... | collective-permute-start | bytes 196616 | tf_op jit(solution)/shard_map/ppermute | solution.py:27
  15.9 4.0 %collective-permute-start.7 = (bf16[2,32,256]{2,1,0:T(8,128)(2,1)S(1)}, bf16[2,32,256]{2,1,0:T(8,128)(2,1)S(1)}, u32[]{:S(2)}, u32[]{:S(2)}) collective-permute-start(bf16[2,32,256]{2,1,0:T(8,128)(2,1)S(1)} %pad_maximum_fusion.3), channel_id=1, source_target_pairs={{0,2},{1,7},{2,0},{3,5},{4,6},{5,3},{6,4},{7,1},{8,10},{9,15},{10,... | collective-permute-start | bytes 98312 | tf_op jit(solution)/shard_map/ppermute | solution.py:27
  19.9 5.6 %collective-permute-start.8 = (bf16[4,32,256]{2,1,0:T(8,128)(2,1)S(1)}, bf16[4,32,256]{2,1,0:T(8,128)(2,1)S(1)}, u32[]{:S(2)}, u32[]{:S(2)}) collective-permute-start(bf16[4,32,256]{2,1,0:T(8,128)(2,1)S(1)} %pad_maximum_fusion.1), channel_id=1, source_target_pairs={{0,6},{1,3},{2,4},{3,1},{4,2},{5,7},{6,0},{7,5},{8,14},{9,11},{10,... | collective-permute-start | bytes 196616 | tf_op jit(solution)/shard_map/ppermute | solution.py:27
  25.5 42.2 %copy-start.2 = (s32[3,16]{1,0:T(4,128)S(1)}, s32[3,16]{1,0:T(4,128)}, u32[]{:S(2)}) copy-start(s32[3,16]{1,0:T(4,128)} %param.10) | copy-start | bytes 580
  25.5 42.3 %copy-start.3 = (s32[3]{0:T(128)S(1)}, s32[3]{0:T(128)}, u32[]{:S(2)}) copy-start(s32[3]{0:T(128)} %param.11) | copy-start | bytes 40
  25.5 65.5 %copy-start = (bf16[1,256,4096]{2,1,0:T(8,128)(2,1)S(1)}, bf16[1,256,4096]{2,1,0:T(8,128)(2,1)}, u32[]{:S(2)}) copy-start(bf16[1,256,4096]{2,1,0:T(8,128)(2,1)} %panel.1) | copy-start | bytes 6291460
  25.6 10.4 %collective-permute-start.9 = (bf16[16,32,256]{2,1,0:T(8,128)(2,1)S(1)}, bf16[16,32,256]{2,1,0:T(8,128)(2,1)S(1)}, u32[]{:S(2)}, u32[]{:S(2)}) collective-permute-start(bf16[16,32,256]{2,1,0:T(8,128)(2,1)S(1)} %get-tuple-element.19), channel_id=1, source_target_pairs={{0,16},{1,49},{2,18},{3,51},{4,20},{5,53},{6,22},{7,55},{8,24},{9,... | collective-permute-start | bytes 786440 | tf_op jit(solution)/shard_map/ppermute | solution.py:27
  36.0 17.5 %collective-permute-start.10 = (bf16[32,32,256]{2,1,0:T(8,128)(2,1)S(1)}, bf16[32,32,256]{2,1,0:T(8,128)(2,1)S(1)}, u32[]{:S(2)}, u32[]{:S(2)}) collective-permute-start(bf16[32,32,256]{2,1,0:T(8,128)(2,1)S(1)} %get-tuple-element.15), channel_id=1, source_target_pairs={{0,48},{1,17},{2,50},{3,19},{4,52},{5,21},{6,54},{7,23},{8,56},{9,... | collective-permute-start | bytes 1572872 | tf_op jit(solution)/shard_map/ppermute | solution.py:27
  53.6 37.5 %collective-permute-start.11 = (bf16[64,32,256]{2,1,0:T(8,128)(2,1)S(1)}, bf16[64,32,256]{2,1,0:T(8,128)(2,1)}, u32[]{:S(2)}, u32[]{:S(2)}) collective-permute-start(bf16[64,32,256]{2,1,0:T(8,128)(2,1)S(1)} %constant_dynamic-update-slice_fusion.17.va), channel_id=1, source_target_pairs={{0,1},{1,0},{2,3},{3,2},{4,5},{5,4},{6,7},{7,6},{8,9},{9,8},{10,11... | collective-permute-start | bytes 3145736 | tf_op jit(solution)/shard_map/ppermute | solution.py:27
  54.2 13.4 %copy-start.1 = (s32[16]{0:T(128)S(1)}, s32[16]{0:T(128)}, u32[]{:S(2)}) copy-start(s32[16]{0:T(128)} %compare_select_fusion.3.meta) | copy-start | bytes 196
  57.6 31.2 %collective-permute-start = (bf16[256,1024]{1,0:T(8,128)(2,1)}, bf16[256,1024]{1,0:T(8,128)(2,1)}, u32[]{:S(2)}, u32[]{:S(2)}) collective-permute-start(bf16[256,1024]{1,0:T(8,128)(2,1)} %get-tuple-element.10), channel_id=1, source_target_pairs={{0,64},{1,65},{2,66},{3,67},{4,68},{5,69},{6,70},{7,71},{8,72},{9,... | collective-permute-start | bytes 1572872 | tf_op jit(solution)/shard_map/ppermute | solution.py:27
  65.5 23.3 %collective-permute-start.1 = (bf16[256,1024]{1,0:T(8,128)(2,1)}, bf16[256,1024]{1,0:T(8,128)(2,1)}, u32[]{:S(2)}, u32[]{:S(2)}) collective-permute-start(bf16[256,1024]{1,0:T(8,128)(2,1)} %get-tuple-element.11), channel_id=1, source_target_pairs={{0,128},{1,129},{2,130},{3,131},{4,132},{5,133},{6,134},{7,135},{8... | collective-permute-start | bytes 1572872 | tf_op jit(solution)/shard_map/ppermute | solution.py:27
  65.5 25.5 %collective-permute-start.2 = (bf16[256,1024]{1,0:T(8,128)(2,1)}, bf16[256,1024]{1,0:T(8,128)(2,1)}, u32[]{:S(2)}, u32[]{:S(2)}) collective-permute-start(bf16[256,1024]{1,0:T(8,128)(2,1)} %get-tuple-element.12), channel_id=1, source_target_pairs={{0,192},{1,193},{2,194},{3,195},{4,196},{5,197},{6,198},{7,199},{8... | collective-permute-start | bytes 1572872 | tf_op jit(solution)/shard_map/ppermute | solution.py:27
  139.8 1.4 collective-permute-start.12
  141.3 4.5 %collective-permute-start.13 = (bf16[16,8,256]{2,1,0:T(8,128)(2,1)S(1)}, bf16[16,8,256]{2,1,0:T(8,128)(2,1)S(1)}, u32[]{:S(2)}, u32[]{:S(2)}) collective-permute-start(bf16[16,8,256]{2,1,0:T(8,128)(2,1)S(1)} %slice.89), channel_id=1, source_target_pairs={{0,2},{1,7},{2,0},{3,5},{4,6},{5,3},{6,4},{7,1},{8,10},{9,15},{10,... | collective-permute-start | bytes 196616 | tf_op jit(solution)/shard_map/ppermute | solution.py:27
  145.9 5.2 %collective-permute-start.14 = (bf16[16,4,256]{2,1,0:T(4,128)(2,1)S(1)}, bf16[16,4,256]{2,1,0:T(4,128)(2,1)S(1)}, u32[]{:S(2)}, u32[]{:S(2)}) collective-permute-start(bf16[16,4,256]{2,1,0:T(4,128)(2,1)S(1)} %slice.90), channel_id=1, source_target_pairs={{0,6},{1,3},{2,4},{3,1},{4,2},{5,7},{6,0},{7,5},{8,14},{9,11},{10,... | collective-permute-start | bytes 98312 | tf_op jit(solution)/shard_map/ppermute | solution.py:27
  151.1 4.2 %collective-permute-start.15 = (f32[8,4,256]{2,1,0:T(4,128)S(1)}, f32[8,4,256]{2,1,0:T(4,128)S(1)}, u32[]{:S(2)}, u32[]{:S(2)}) collective-permute-start(f32[8,4,256]{2,1,0:T(4,128)S(1)} %slice.71), channel_id=1, source_target_pairs={{0,64},{1,193},{2,66},{3,195},{4,68},{5,197},{6,70},{7,199},{8,72}... | collective-permute-start | bytes 98312 | tf_op jit(solution)/shard_map/ppermute | solution.py:27
  155.3 3.8 %collective-permute-start.16 = (f32[4,4,256]{2,1,0:T(4,128)S(1)}, f32[4,4,256]{2,1,0:T(4,128)S(1)}, u32[]{:S(2)}, u32[]{:S(2)}) collective-permute-start(f32[4,4,256]{2,1,0:T(4,128)S(1)} %slice.73), channel_id=1, source_target_pairs={{0,192},{1,65},{2,194},{3,67},{4,196},{5,69},{6,198},{7,71},{8,200... | collective-permute-start | bytes 49160 | tf_op jit(solution)/shard_map/ppermute | solution.py:27
  159.1 4.6 %collective-permute-start.17 = (f32[4,2,256]{2,1,0:T(2,128)S(1)}, f32[4,2,256]{2,1,0:T(2,128)S(1)}, u32[]{:S(2)}, u32[]{:S(2)}) collective-permute-start(f32[4,2,256]{2,1,0:T(2,128)S(1)} %slice.75), channel_id=1, source_target_pairs={{0,8},{1,9},{2,10},{3,11},{4,12},{5,13},{6,14},{7,15},{8,0},{9,1},... | collective-permute-start | bytes 24584 | tf_op jit(solution)/shard_map/ppermute | solution.py:27
  163.7 4.6 %collective-permute-start.18 = (f32[2,2,256]{2,1,0:T(2,128)S(1)}, f32[2,2,256]{2,1,0:T(2,128)S(1)}, u32[]{:S(2)}, u32[]{:S(2)}) collective-permute-start(f32[2,2,256]{2,1,0:T(2,128)S(1)} %slice.77), channel_id=1, source_target_pairs={{0,16},{1,49},{2,18},{3,51},{4,20},{5,53},{6,22},{7,55},{8,24},{9,... | collective-permute-start | bytes 12296 | tf_op jit(solution)/shard_map/ppermute | solution.py:27
  168.3 5.7 %collective-permute-start.19 = (f32[1,2,256]{2,1,0:T(2,128)S(1)}, f32[1,2,256]{2,1,0:T(2,128)S(1)}, u32[]{:S(2)}, u32[]{:S(2)}) collective-permute-start(f32[1,2,256]{2,1,0:T(2,128)S(1)} %slice.79), channel_id=1, source_target_pairs={{0,48},{1,17},{2,50},{3,19},{4,52},{5,21},{6,54},{7,23},{8,56},{9,... | collective-permute-start | bytes 6152 | tf_op jit(solution)/shard_map/ppermute | solution.py:27
